TPU v7x, 256 devices: a whole 4x4x8 slice. The times are simulated.
256 devices in a mesh: grp: 4 (over y), curve: 64 (over z, x, core).
Axes of the slice: x: 4, y: 4, z: 8, core: 2. Of those that a mesh axis runs over, the one named last changes fastest.
Arguments:
- adjoint: float32 [4, 9, 84, 8192], P('grp', None, None, 'curve'), may hold values from -6 to 6
- forward: float32 [2, 4, 9, 84, 8192], P(None, 'grp', None, None, 'curve'), may hold values from -6 to 6
- star_mats: float32 [3, 81, 8192], P(None, None, 'curve'), may hold values from -2 to 2
- flux_own: float32 [4, 81, 8192], P(None, None, 'curve'), may hold values from -2 to 2
- flux_neighbour: float32 [4, 81, 8192], P(None, None, 'curve'), may hold values from -2 to 2
- stiffness: float32 [3, 84, 84], replicated, may hold values from -0.625 to 0.625
- projection: float32 [112, 84], replicated, may hold values from -0.625 to 0.625
- lifting: float32 [4, 84, 28], replicated, may hold values from -0.5 to 0.5
- orientation: float32 [3, 28, 28], replicated, may hold values from -1 to 1
- face_turn: int32 [4, 8192], P(None, 'curve'), may hold values from 0 to 2
- mass_weights: float32 [84], replicated, may hold values from 0.005 to 0.05
- param_mixing: float32 [3, 81], replicated, may hold values from -0.625 to 0.625
- neighbour: int32 [4, 8192], P(None, 'curve'), may hold values from 0 to 768, as said below
- send_map: int32 [2, 8192], P(None, 'curve'), may hold values from 0 to 512, as said below
- element_cell: int32 [8192], P('curve'), may hold values from 0 to 32767, as said below
Outputs:
- adjoint_out: float32 [4, 9, 84, 8192], P('grp', None, None, 'curve')
- kernel_tiles: float32 [256, 3, 128], P(('grp', 'curve'))
Inputs may be any that keep to these rules, and one draw needn't show every extreme that they name: `neighbour`: entry [i, c] locates the face adjacent to face i of cell c: below 512 it is the face pointer of a face of the same device, from 512 to 639 a slot sent by the previous device of curve, up to 767 a slot sent by the next device, and 768 a face on the boundary of the slab. `send_map`: each device's block of 128 entries per row holds face pointers of that device's faces in its leading live slots and 512 in the empty ones; at least half of the slots are live, and in each row some device fills all 128. `element_cell`: A cell held by device k of curve lies in a tile u whose position u modulo the number of curve devices is k - 1, k or k + 1; the tile's group u divided by that number may be any.
All inputs are finite; a program needn't handle non-finite values.
Results may differ from a plain program's by a relative error of at most 0.0001.
Values sent between devices are 32-bit elements; how exact they have to be, the bound alone decides.
A program may use at most 128 MiB of HBM per device.

v0:
```python
import jax
import jax.numpy as jnp
from jax import lax
from jax.experimental import pallas as pl
from jax.experimental.pallas import tpu as pltpu
from jax.experimental.layout import Layout, with_layout_constraint
from jax.sharding import PartitionSpec as P

TERMS = 3
STEPS = 2
TILE = 128


PRECISE = lax.Precision.HIGHEST
TIME_STEP = 0.4


def star(matrix, values):
    m3 = matrix.reshape(9, 9, *matrix.shape[1:])
    out = m3[:, 0][:, None] * values[0][None]
    for source in range(1, 9):
        out = out + m3[:, source][:, None] * values[source][None]
    return out


def star_sum(mats, moved):
    out = star(mats[0], moved[0])
    for axis_dir in (1, 2):
        out = out + star(mats[axis_dir], moved[axis_dir])
    return out


def predictor(state, stiffness, star_mats):
    derivative = state
    factor = TIME_STEP
    integral = factor * state
    for degree in range(1, TERMS):
        moved = jnp.einsum("dab,qbc->dqac", stiffness, derivative, precision=PRECISE)
        derivative = star_sum(star_mats, moved)
        factor = factor * TIME_STEP / (degree + 1)
        integral = integral + factor * derivative
    return integral


def volume(integral, stiffness, star_mats):
    moved = jnp.einsum("dba,qbc->dqac", stiffness, integral, precision=PRECISE)
    return star_sum(star_mats, moved)


def turn_faces(gathered, orientation, face_turn):
    turned = jnp.einsum("rts,qsic->rqtic", orientation, gathered, precision=PRECISE)
    result = jnp.zeros_like(gathered)
    for turn_index in range(3):
        result = result + jnp.where(face_turn[None, None] == turn_index, turned[turn_index], 0.0)
    return result


def exchange_kernel(count, to_next, to_prev, from_prev, from_next, send_sem, recv_sem):
    group = lax.axis_index("grp")
    me = lax.axis_index("curve")
    right, left = lax.rem(me + 1, count), lax.rem(me + count - 1, count)
    barrier = pltpu.get_barrier_semaphore()
    for side in (left, right):
        pl.semaphore_signal(barrier, inc=1, device_id=(group, side), device_id_type=pl.DeviceIdType.MESH)
    pl.semaphore_wait(barrier, 2)
    copies = [
        pltpu.make_async_remote_copy(
            src_ref=to_next,
            dst_ref=from_prev,
            send_sem=send_sem.at[0],
            recv_sem=recv_sem.at[0],
            device_id=(group, right),
            device_id_type=pl.DeviceIdType.MESH,
        ),
        pltpu.make_async_remote_copy(
            src_ref=to_prev,
            dst_ref=from_next,
            send_sem=send_sem.at[1],
            recv_sem=recv_sem.at[1],
            device_id=(group, left),
            device_id_type=pl.DeviceIdType.MESH,
        ),
    ]
    for copy in copies:
        copy.start()
    for copy in copies:
        copy.wait()


def exchange(to_next, to_prev):
    count = lax.axis_size("curve")
    me = lax.axis_index("curve")
    vmem = pl.BlockSpec(memory_space=pltpu.VMEM)
    from_prev, from_next = pl.pallas_call(
        lambda *refs: exchange_kernel(count, *refs),
        out_shape=(jax.ShapeDtypeStruct(to_next.shape, to_next.dtype),) * 2,
        in_specs=[vmem, vmem],
        out_specs=(vmem, vmem),
        scratch_shapes=[pltpu.SemaphoreType.DMA((2,)), pltpu.SemaphoreType.DMA((2,))],
        compiler_params=pltpu.CompilerParams(collective_id=0, has_side_effects=True),
    )(to_next, to_prev)
    from_prev = jnp.where(me == 0, 0.0, from_prev)
    from_next = jnp.where(me == count - 1, 0.0, from_next)
    return from_prev, from_next


def scatter_kernel(offsets, group_count, curve_count, chunks, received, send_sem, recv_sem):
    group = lax.axis_index("grp")
    me = lax.axis_index("curve")
    targets = [
        (lax.rem(group + shift_group, group_count), lax.rem(me + shift_curve + curve_count, curve_count))
        for shift_group, shift_curve in offsets
    ]
    barrier = pltpu.get_barrier_semaphore()
    for target in targets:
        pl.semaphore_signal(barrier, inc=1, device_id=target, device_id_type=pl.DeviceIdType.MESH)
    pl.semaphore_wait(barrier, len(offsets))
    copies = [
        pltpu.make_async_remote_copy(
            src_ref=chunks.at[index],
            dst_ref=received.at[index],
            send_sem=send_sem.at[index],
            recv_sem=recv_sem.at[index],
            device_id=target,
            device_id_type=pl.DeviceIdType.MESH,
        )
        for index, target in enumerate(targets)
    ]
    for copy in copies:
        copy.start()
    for copy in copies:
        copy.wait()


def scatter_tiles(partial):
    group_count = lax.axis_size("grp")
    curve_count = lax.axis_size("curve")
    offsets = [
        (shift_group, shift_curve)
        for shift_group in range(group_count)
        for shift_curve in (-1, 0, 1)
        if (shift_group, shift_curve) != (0, 0)
    ]
    chunks = jnp.stack([partial[:, g, c + 1] for g, c in offsets])
    vmem = pl.BlockSpec(memory_space=pltpu.VMEM)
    received = pl.pallas_call(
        lambda *refs: scatter_kernel(offsets, group_count, curve_count, *refs),
        out_shape=jax.ShapeDtypeStruct(chunks.shape, chunks.dtype),
        in_specs=[vmem],
        out_specs=vmem,
        scratch_shapes=[
            pltpu.SemaphoreType.DMA((len(offsets),)),
            pltpu.SemaphoreType.DMA((len(offsets),)),
        ],
        compiler_params=pltpu.CompilerParams(collective_id=1, has_side_effects=True),
    )(chunks)
    return partial[:, 0, 1] + jnp.sum(received, axis=0)


def on_device(
    adjoint,
    forward,
    star_mats,
    flux_own,
    flux_neighbour,
    stiffness,
    projection,
    lifting,
    orientation,
    face_turn,
    mass_weights,
    param_mixing,
    neighbour,
    send_map,
    element_cell,
):
    cells = adjoint.shape[3]
    basis = adjoint.shape[2]
    slots = send_map.shape[1]
    face_basis = projection.shape[0] // 4
    curve_count = lax.axis_size("curve")
    group_count = lax.axis_size("grp")
    my_curve = lax.axis_index("curve")
    my_group = lax.axis_index("grp")
    f32 = jnp.float32

    own_flux = jnp.transpose(flux_own, (1, 0, 2))
    far_flux = jnp.transpose(flux_neighbour, (1, 0, 2))
    face_proj = projection.reshape(4, face_basis, basis)
    rows = 9 * face_basis

    faces = jnp.arange(4 * cells, dtype=jnp.int32)
    send_oh = (faces[:, None] == jnp.concatenate([send_map[0], send_map[1]])[None, :]).astype(f32)
    table_cols = jnp.arange(4 * cells + 2 * slots, dtype=jnp.int32)
    gather_oh = (table_cols[:, None] == neighbour.reshape(-1)[None, :]).astype(f32)

    mix = param_mixing.reshape(3, 9, 9)
    state = with_layout_constraint(
        adjoint.reshape(adjoint.shape[1:]), Layout((0, 1, 2))
    )
    density_sum = jnp.zeros((3, cells), f32)
    for time_step in range(STEPS):
        integral = predictor(state, stiffness, star_mats)
        own_trace = jnp.einsum("itb,qbc->qtic", face_proj, integral, precision=PRECISE)
        table = own_trace.reshape(rows, 4 * cells)
        outgoing = jnp.dot(table, send_oh, precision=PRECISE)
        from_prev, from_next = exchange(outgoing[:, slots:], outgoing[:, :slots])
        volume_term = volume(integral, stiffness, star_mats)
        extended = jnp.concatenate([table, from_prev, from_next], axis=1)
        gathered = jnp.dot(extended, gather_oh, precision=PRECISE).reshape(9, face_basis, 4, cells)
        oriented = turn_faces(gathered, orientation, face_turn)
        face_flux = star(own_flux, own_trace) + star(far_flux, oriented)
        lifted = jnp.einsum("ibt,qtic->qbc", lifting, face_flux, precision=PRECISE)
        state = state + volume_term - lifted
        weighted = state * mass_weights[None, :, None]
        mixed = jnp.einsum("pqr,rbc->pqbc", mix, forward[time_step, 0], precision=PRECISE)
        density_sum = density_sum + jnp.sum(weighted[None] * mixed, axis=(1, 2))

    tile = element_cell // TILE
    inside = element_cell % TILE
    rel_group = (tile // curve_count - my_group) % group_count
    rel_curve = (tile % curve_count - my_curve + 1) % curve_count
    slot = (rel_group * 3 + rel_curve) * TILE + inside
    slot = jnp.where(rel_curve < 3, slot, -1)
    tile_oh = (slot[:, None] == jnp.arange(group_count * 3 * TILE, dtype=jnp.int32)[None, :]).astype(f32)
    partial = jnp.dot(density_sum, tile_oh, precision=PRECISE).reshape(3, group_count, 3, TILE)

    kernel = scatter_tiles(partial)
    return (state.reshape(adjoint.shape), kernel[None])


def solution(mesh):
    return jax.shard_map(
        on_device,
        mesh=mesh,
        in_specs=(
            P("grp", None, None, "curve"),
            P(None, "grp", None, None, "curve"),
            P(None, None, "curve"),
            P(None, None, "curve"),
            P(None, None, "curve"),
            P(),
            P(),
            P(),
            P(),
            P(None, "curve"),
            P(),
            P(),
            P(None, "curve"),
            P(None, "curve"),
            P("curve"),
        ),
        out_specs=(P("grp", None, None, "curve"), P(("grp", "curve"), None, None)),
        check_vma=False,
    )
```

profile of v0, /device:TPU:1, one launch (start us, length us, event | category | flops | bytes accessed | tf_op | source)
XLA Modules:
  0.0 81.4 jit_solution(5431539030914359627)
XLA Ops:
  0.7 0.9 %fusion.215 = (f32[1,81,128]{2,1,0:T(8,128)S(1)}, f32[1,81,128]{2,1,0:T(8,128)S(1)}, f32[1,81,128]{2,1,0:T(8,128)S(1)}) fusion(f32[3,81,128]{2,1,0:T(8,128)} %param.17), kind=kLoop, calls=%fused_computation.540 | loop fusion | bytes 248832 | tf_op jit(solution)/shard_map/slice | solution.py:27
  1.9 1.2 %convolution_bitcast_fusion.7 = f32[3,9,84,128]{3,2,0,1:T(8,128)S(1)} fusion(f32[1,9,84,128]{3,0,2,1:T(1,128)S(1)} %copy-done.1, f32[3,84,84]{2,1,0:T(8,128)S(1)} %copy-done), kind=kOutput, calls=%fused_computation.12 | convolution fusion | flops 292626432 | bytes 1632960 | tf_op jit(solution)/shard_map/dab,qbc->dqac/dot_general | solution.py:38
  3.1 0.1 slice_bitcast_fusion.203
  3.2 2.4 %convolution_bitcast_fusion.6 = f32[3,9,84,128]{3,2,0,1:T(8,128)S(1)} fusion(f32[3,84,84]{2,1,0:T(8,128)S(1)} %copy-done, f32[84,128]{1,0:T(8,128)S(1)} %get-tuple-element.152, f32[9,128]{1,0:T(8,128)S(1)} %get-tuple-element.276, f32[84,128]{1,0:T(8,128)S(1)} %get-tuple-element.153, f32[9,128]{1,0:T(8,128)S(1)} %get-tuple-element.277, ...), kind=kOutput, calls=%fused_computation.11 | convolution fusion | flops 297755136 | bytes 2531520 | tf_op jit(solution)/shard_map/dab,qbc->dqac/dot_general | solution.py:38
  5.6 0.1 slice_bitcast_fusion.176
  5.8 2.3 %fusion.105 = f32[9,84,128,1]{2,1,3,0:T(8,128)S(1)} fusion(f32[1,9,84,128]{3,0,2,1:T(1,128)S(1)} %copy-done.1, f32[84,128]{1,0:T(8,128)S(1)} %get-tuple-element.125, f32[84,128]{1,0:T(8,128)S(1)} %get-tuple-element.126, f32[84,128]{1,0:T(8,128)S(1)} %get-tuple-element.127, f32[84,128]{1,0:T(8,128)S(1)} %get-tuple-element.128, ...), kind=kLoop, calls=%fused_computation.132 | loop fusion | flops 10741248 | bytes 3220992 | tf_op jit(solution)/shard_map/add | solution.py:41
  8.0 0.1 copy.126
  8.1 0.6 convolution_bitcast_fusion.9
  8.8 0.3 copy.127
  9.2 0.1 pad.8
  9.3 0.5 copy-done.28
  9.8 0.4 fusion.101
  10.3 0.7 fusion.214
  11.0 11.5 %shard_map.158 = (f32[252,128]{1,0:T(8,128)}, f32[252,128]{1,0:T(8,128)}) custom-call(f32[252,128]{1,0:T(8,128)} %get-tuple-element.219.refs_0_, f32[252,128]{1,0:T(8,128)} %get-tuple-element.218.refs_1_), custom_call_target="tpu_custom_call" | custom-call | tf_op jit(solution)/shard_map/pallas_call | solution.py:94
  22.6 0.9 %broadcast_select_fusion.2 = f32[252,128]{1,0:T(8,128)S(1)} fusion(f32[252,128]{1,0:T(8,128)} %get-tuple-element.7, pred[]{:T(512)S(6)} %eq.74), kind=kLoop, calls=%fused_computation.267 | loop fusion | flops 32256 | bytes 258049 | tf_op jit(solution)/shard_map/jit(_where)/select_n | solution.py:103
  23.5 0.9 %broadcast_select_fusion.3 = f32[252,128]{1,0:T(8,128)S(1)} fusion(f32[252,128]{1,0:T(8,128)} %get-tuple-element.6, pred[]{:T(512)S(6)} %eq.70), kind=kLoop, calls=%fused_computation.268 | loop fusion | flops 32256 | bytes 258049 | tf_op jit(solution)/shard_map/jit(_where)/select_n | solution.py:102
  24.4 0.9 %fusion.1 = f32[252,512]{1,0:T(8,128)S(1)} fusion(f32[252,128]{1,0:T(8,128)S(1)} %broadcast_select_fusion.2, f32[252,128]{1,0:T(8,128)S(1)} %broadcast_select_fusion.3, f32[252,512]{1,0:T(8,128)S(1)} %bitcast.737, s32[512]{0:T(512)S(1)} %bitcast.765), kind=kOutput, calls=%fused_computation.4 | convolution fusion | flops 1189865472 | bytes 1292288 | tf_op jit(solution)/shard_map/dot_general | solution.py:210
  25.4 0.2 reshape.394
  25.6 1.5 %convolution_bitcast_fusion.1 = f32[3,9,28,4,128]{4,2,0,3,1:T(8,128)S(1)} fusion(f32[9,28,4,128,1]{3,2,1,0,4:T(4,128)S(1)} %bitcast.735, f32[3,28,28]{2,1,0:T(8,128)S(1)} %copy-done.3), kind=kOutput, calls=%fused_computation.6 | convolution fusion | flops 130056192 | bytes 2073792 | tf_op jit(solution)/shard_map/rts,qsic->rqtic/dot_general | solution.py:51
  27.2 0.2 fusion.23
  27.4 0.3 copy-done.20
  27.7 0.0 copy-done.24
  27.7 1.3 %convolution_bitcast_fusion.5 = f32[3,9,84,128]{3,2,0,1:T(8,128)S(1)} fusion(f32[9,84,128,1]{2,1,3,0:T(8,128)S(1)} %fusion.105, f32[3,84,84]{2,1,0:T(8,128)S(1)} %copy-done), kind=kOutput, calls=%fused_computation.10 | convolution fusion | flops 292626432 | bytes 1632960 | tf_op jit(solution)/shard_map/dba,qbc->dqac/dot_general | solution.py:46
  29.0 0.1 slice_bitcast_fusion.149
  29.2 0.8 copy-done.4
  30.0 0.1 copy-done.5
  30.1 0.2 slice_bitcast_fusion.212
  30.3 2.7 %fusion.2 = f32[9,84,128]{2,1,0:T(8,128)S(1)} fusion(f32[1,9,84,128]{3,0,2,1:T(1,128)S(1)} %copy-done.1, f32[28,4,128]{2,0,1:T(8,128)S(1)} %get-tuple-element.208, f32[9,4,128]{2,1,0:T(4,128)S(1)} %get-tuple-element.230, f32[28,4,128]{2,0,1:T(8,128)S(1)} %get-tuple-element.209, f32[9,4,128]{2,1,0:T(4,128)S(1)} %get-tuple-element.231, ...), kind=kOutput, calls=%fused_computation.17 | convolution fusion | flops 139894272 | bytes 3461376 | tf_op jit(solution)/shard_map/ibt,qtic->qbc/dot_general | solution.py:213
  33.0 1.2 %convolution_bitcast_fusion.4 = f32[3,9,84,128]{3,2,0,1:T(8,128)S(1)} fusion(f32[9,84,128]{2,1,0:T(8,128)S(1)} %fusion.2, f32[3,84,84]{2,1,0:T(8,128)S(1)} %copy-done), kind=kOutput, calls=%fused_computation.9 | convolution fusion | flops 292626432 | bytes 1632960 | tf_op jit(solution)/shard_map/dab,qbc->dqac/dot_general | solution.py:38
  34.2 0.1 slice_bitcast_fusion.122
  34.4 2.4 %convolution_bitcast_fusion.3 = f32[3,9,84,128]{3,2,0,1:T(8,128)S(1)} fusion(f32[3,84,84]{2,1,0:T(8,128)S(1)} %copy-done, f32[84,128]{1,0:T(8,128)S(1)} %get-tuple-element.71, f32[84,128]{1,0:T(8,128)S(1)} %get-tuple-element.72, f32[84,128]{1,0:T(8,128)S(1)} %get-tuple-element.73, f32[84,128]{1,0:T(8,128)S(1)} %get-tuple-element.74, ...), kind=kOutput, calls=%fused_computation.8 | convolution fusion | flops 297755136 | bytes 2531520 | tf_op jit(solution)/shard_map/dab,qbc->dqac/dot_general | solution.py:38
  36.8 0.1 slice_bitcast_fusion.95
  36.9 2.3 %multiply_add_fusion = f32[9,84,128]{2,1,0:T(8,128)S(1)} fusion(f32[9,84,128]{2,1,0:T(8,128)S(1)} %fusion.2, f32[84,128]{1,0:T(8,128)S(1)} %get-tuple-element.44, f32[84,128]{1,0:T(8,128)S(1)} %get-tuple-element.45, f32[84,128]{1,0:T(8,128)S(1)} %get-tuple-element.46, f32[84,128]{1,0:T(8,128)S(1)} %get-tuple-element.47, ...), kind=kLoop, calls=%fused_computation.138 | loop fusion | flops 10741248 | bytes 3220992 | tf_op jit(solution)/shard_map/add | solution.py:41
  39.2 0.6 convolution_bitcast_fusion.8
  39.8 0.3 copy.133
  40.2 0.1 pad.9
  40.3 0.4 fusion.100
  40.8 0.7 fusion.213
  41.5 8.5 %shard_map.159 = (f32[252,128]{1,0:T(8,128)}, f32[252,128]{1,0:T(8,128)}) custom-call(f32[252,128]{1,0:T(8,128)} %get-tuple-element.217.refs_0_, f32[252,128]{1,0:T(8,128)} %get-tuple-element.216.refs_1_), custom_call_target="tpu_custom_call" | custom-call | tf_op jit(solution)/shard_map/pallas_call | solution.py:94
  50.0 0.9 %broadcast_select_fusion.1 = f32[252,128]{1,0:T(8,128)S(1)} fusion(f32[252,128]{1,0:T(8,128)} %get-tuple-element.8, pred[]{:T(512)S(6)} %eq.70), kind=kLoop, calls=%fused_computation.266 | loop fusion | flops 32256 | bytes 258049 | tf_op jit(solution)/shard_map/jit(_where)/select_n | solution.py:102
  50.9 0.9 %broadcast_select_fusion = f32[252,128]{1,0:T(8,128)S(1)} fusion(f32[252,128]{1,0:T(8,128)} %get-tuple-element.9, pred[]{:T(512)S(6)} %eq.74), kind=kLoop, calls=%fused_computation.265 | loop fusion | flops 32256 | bytes 258049 | tf_op jit(solution)/shard_map/jit(_where)/select_n | solution.py:103
  51.9 0.9 %fusion = f32[252,512]{1,0:T(8,128)S(1)} fusion(f32[252,128]{1,0:T(8,128)S(1)} %broadcast_select_fusion, f32[252,128]{1,0:T(8,128)S(1)} %broadcast_select_fusion.1, f32[252,512]{1,0:T(8,128)S(1)} %bitcast.739, s32[512]{0:T(512)S(1)} %bitcast.766), kind=kOutput, calls=%fused_computation.3 | convolution fusion | flops 1189865472 | bytes 1292288 | tf_op jit(solution)/shard_map/dot_general | solution.py:210
  52.8 0.2 reshape.396
  53.0 1.8 %convolution_bitcast_fusion = f32[3,9,28,4,128]{4,2,3,1,0:T(8,128)S(1)} fusion(f32[9,28,4,128]{3,2,1,0:T(4,128)S(1)} %reshape.396, f32[3,28,28]{2,1,0:T(8,128)S(1)} %copy-done.3), kind=kOutput, calls=%fused_computation.5 | convolution fusion | flops 130056192 | bytes 2073792 | tf_op jit(solution)/shard_map/rts,qsic->rqtic/dot_general | solution.py:51
  54.8 0.2 fusion.18
  55.1 1.3 %convolution_bitcast_fusion.2 = f32[3,9,84,128]{3,2,0,1:T(8,128)S(1)} fusion(f32[9,84,128]{2,1,0:T(8,128)S(1)} %multiply_add_fusion, f32[3,84,84]{2,1,0:T(8,128)S(1)} %copy-done), kind=kOutput, calls=%fused_computation.7 | convolution fusion | flops 292626432 | bytes 1632960 | tf_op jit(solution)/shard_map/dba,qbc->dqac/dot_general | solution.py:46
  56.4 0.1 slice_bitcast_fusion.68
  56.6 0.6 copy-done.9
  57.1 0.0 copy-done.11
  57.2 0.1 copy-done.31
  57.3 2.7 %broadcast_multiply_fusion = (f32[9,84,128]{2,1,0:T(8,128)S(1)}, f32[9,84,128]{2,1,0:T(8,128)S(1)}, f32[9,84,128]{2,1,0:T(8,128)S(1)}) fusion(f32[84]{0:T(128)S(1)} %copy-done.34, f32[9,84,128]{2,1,0:T(8,128)S(1)} %fusion.2, f32[4,84,28]{1,0,2:T(4,128)S(1)} %copy-done.31, f32[28,4,128]{2,0,1:T(8,128)S(1)} %get-tuple-element.190, ...), kind=kOutput, calls=%fused_computation.217 | convolution fusion | flops 140087808 | bytes 4235856 | tf_op jit(solution)/shard_map/ibt,qtic->qbc/dot_general | solution.py:213
  60.0 0.1 copy.140
  60.2 1.0 %copy-done.2 = f32[2,1,9,84,128]{4,1,3,2,0:T(1,128)S(1)} copy-done((f32[2,1,9,84,128]{4,1,3,2,0:T(1,128)S(1)}, f32[2,1,9,84,128]{4,1,3,2,0:T(1,128)}, u32[]{:S(2)}) %copy-start.2) | copy-done | bytes 774168
  61.1 0.1 fusion.212
  61.2 0.1 reshape.417
  61.3 1.8 %multiply_reduce_fusion = f32[3,128]{1,0:T(4,128)S(1)} fusion(f32[9,84,128]{2,0,1:T(8,128)S(1)} %copy.140, f32[1,1,9,84,128]{4,1,3,2,0:T(1,128)S(1)} %get-tuple-element.178, f32[3,9,9,1]{2,1,0,3:T(8,128)S(1)} %reshape.417), kind=kOutput, calls=%fused_computation | convolution fusion | flops 31933056 | bytes 776652 | tf_op jit(solution)/shard_map/pqr,rbc->pqbc/dot_general | solution.py:216
  63.1 0.1 copy.137
  63.3 1.8 %multiply_reduce_fusion.1 = f32[3,128]{1,0:T(4,128)S(1)} fusion(f32[9,84,128]{2,0,1:T(8,128)S(1)} %copy.137, f32[1,1,9,84,128]{4,1,3,2,0:T(1,128)S(1)} %get-tuple-element.179, f32[3,9,9,1]{2,1,0,3:T(8,128)S(1)} %reshape.417), kind=kOutput, calls=%fused_computation.1 | convolution fusion | flops 31933056 | bytes 776652 | tf_op jit(solution)/shard_map/pqr,rbc->pqbc/dot_general | solution.py:216
  65.2 0.4 fusion.16
  65.7 0.6 copy-done.7
  66.3 12.6 %shard_map.160 = f32[11,3,128]{2,1,0:T(4,128)} custom-call(f32[11,3,128]{2,1,0:T(4,128)} %copy-done.7), custom_call_target="tpu_custom_call" | custom-call | tf_op jit(solution)/shard_map/pallas_call | solution.py:146
  78.9 0.8 reduce_sum.31
  79.7 0.6 copy.144
  80.2 1.1 %copy.143 = f32[1,9,84,128]{3,0,2,1:T(1,128)} copy(f32[1,9,84,128]{3,2,1,0:T(8,128)S(1)} %bitcast.744) | data formatting | bytes 774144
  (109 shorter events, 0.9 us)
Async XLA Ops:
  0.6 1.2 %copy-start = (f32[3,84,84]{2,1,0:T(8,128)S(1)}, f32[3,84,84]{2,1,0:T(8,128)}, u32[]{:S(2)}) copy-start(f32[3,84,84]{2,1,0:T(8,128)} %param.20) | copy-start | bytes 254020
  0.6 1.2 %copy-start.1 = (f32[1,9,84,128]{3,0,2,1:T(1,128)S(1)}, f32[1,9,84,128]{3,0,2,1:T(1,128)}, u32[]{:S(2)}) copy-start(f32[1,9,84,128]{3,0,2,1:T(1,128)} %param.15) | copy-start | bytes 1161220
  5.7 2.3 %copy-start.6 = (f32[112,84]{0,1:T(8,128)S(1)}, f32[112,84]{0,1:T(8,128)}, u32[]{:S(2)}) copy-start(f32[112,84]{0,1:T(8,128)} %param.21) | copy-start | bytes 112900
  9.1 0.7 copy-start.28
  9.3 15.1 %copy-start.32 = (s32[4,128]{1,0:T(4,128)S(1)}, s32[4,128]{1,0:T(4,128)}, u32[]{:S(2)}) copy-start(s32[4,128]{1,0:T(4,128)} %param.27) | copy-start | bytes 6148
  24.4 1.2 %copy-start.3 = (f32[3,28,28]{2,1,0:T(8,128)S(1)}, f32[3,28,28]{2,1,0:T(8,128)}, u32[]{:S(2)}) copy-start(f32[3,28,28]{2,1,0:T(8,128)} %param.23) | copy-start | bytes 28228
  25.6 1.6 %copy-start.26 = (s32[4,128]{1,0:T(4,128)S(1)}, s32[4,128]{1,0:T(4,128)}, u32[]{:S(2)}) copy-start(s32[4,128]{1,0:T(4,128)} %param.24) | copy-start | bytes 6148
  27.1 0.6 copy-start.20
  27.1 0.6 copy-start.22
  27.2 0.6 copy-start.24
  29.1 0.9 %copy-start.4 = (f32[4,81,128]{2,0,1:T(4,128)S(1)}, f32[4,81,128]{2,0,1:T(4,128)}, u32[]{:S(2)}) copy-start(f32[4,81,128]{2,0,1:T(4,128)} %param.19) | copy-start | bytes 497668
  29.1 1.0 %copy-start.5 = (f32[4,81,128]{2,0,1:T(4,128)S(1)}, f32[4,81,128]{2,0,1:T(4,128)}, u32[]{:S(2)}) copy-start(f32[4,81,128]{2,0,1:T(4,128)} %param.18) | copy-start | bytes 497668
  29.1 1.2 %copy-start.30 = (f32[4,84,28]{1,0,2:T(4,128)S(1)}, f32[4,84,28]{1,0,2:T(4,128)}, u32[]{:S(2)}) copy-start(f32[4,84,28]{1,0,2:T(4,128)} %param.22) | copy-start | bytes 112900
  30.2 2.7 %copy-start.8 = (f32[9,4,128]{2,1,0:T(4,128)}, f32[9,4,128]{2,1,0:T(4,128)S(1)}, u32[]{:S(2)}) copy-start(f32[9,4,128]{2,1,0:T(4,128)S(1)} %get-tuple-element.305) | copy-start | bytes 55300
  30.2 2.7 %copy-start.10 = (f32[9,4,128]{2,1,0:T(4,128)}, f32[9,4,128]{2,1,0:T(4,128)S(1)}, u32[]{:S(2)}) copy-start(f32[9,4,128]{2,1,0:T(4,128)S(1)} %get-tuple-element.306) | copy-start | bytes 55300
  30.3 2.7 %copy-start.12 = (f32[9,4,128]{2,1,0:T(4,128)}, f32[9,4,128]{2,1,0:T(4,128)S(1)}, u32[]{:S(2)}) copy-start(f32[9,4,128]{2,1,0:T(4,128)S(1)} %get-tuple-element.307) | copy-start | bytes 55300
  30.3 2.7 %copy-start.14 = (f32[9,4,128]{2,1,0:T(4,128)}, f32[9,4,128]{2,1,0:T(4,128)S(1)}, u32[]{:S(2)}) copy-start(f32[9,4,128]{2,1,0:T(4,128)S(1)} %get-tuple-element.308) | copy-start | bytes 55300
  30.3 2.7 %copy-start.16 = (f32[9,4,128]{2,1,0:T(4,128)}, f32[9,4,128]{2,1,0:T(4,128)S(1)}, u32[]{:S(2)}) copy-start(f32[9,4,128]{2,1,0:T(4,128)S(1)} %get-tuple-element.309) | copy-start | bytes 55300
  30.3 2.7 %copy-start.18 = (f32[9,4,128]{2,1,0:T(4,128)}, f32[9,4,128]{2,1,0:T(4,128)S(1)}, u32[]{:S(2)}) copy-start(f32[9,4,128]{2,1,0:T(4,128)S(1)} %get-tuple-element.310) | copy-start | bytes 55300
  40.3 11.6 %copy-start.33 = (s32[4,128]{1,0:T(4,128)S(1)}, s32[4,128]{1,0:T(4,128)}, u32[]{:S(2)}) copy-start(s32[4,128]{1,0:T(4,128)} %param.27) | copy-start | bytes 6148
  53.0 1.8 %copy-start.21 = (pred[4,128]{1,0:T(4,128)(4,1)S(1)}, pred[4,128]{1,0:T(4,128)(4,1)}, u32[]{:S(2)}) copy-start(pred[4,128]{1,0:T(4,128)(4,1)} %copy-done.20) | copy-start | bytes 1540
  53.0 1.8 %copy-start.23 = (pred[4,128]{1,0:T(4,128)(4,1)S(1)}, pred[4,128]{1,0:T(4,128)(4,1)}, u32[]{:S(2)}) copy-start(pred[4,128]{1,0:T(4,128)(4,1)} %copy-done.22) | copy-start | bytes 1540
  53.0 1.8 %copy-start.25 = (pred[4,128]{1,0:T(4,128)(4,1)S(1)}, pred[4,128]{1,0:T(4,128)(4,1)}, u32[]{:S(2)}) copy-start(pred[4,128]{1,0:T(4,128)(4,1)} %copy-done.24) | copy-start | bytes 1540
  56.4 0.7 copy-start.9
  56.4 0.7 copy-start.11
  56.4 0.7 copy-start.13
  56.5 0.7 copy-start.15
  56.5 0.8 copy-start.17
  56.5 0.8 copy-start.19
  56.5 0.9 %copy-start.31 = (f32[4,84,28]{1,0,2:T(4,128)S(1)}, f32[4,84,28]{1,0,2:T(4,128)}, u32[]{:S(2)}) copy-start(f32[4,84,28]{1,0,2:T(4,128)} %param.22) | copy-start | bytes 112900
  56.5 0.9 %copy-start.34 = (f32[84]{0:T(128)S(1)}, f32[84]{0:T(128)}, u32[]{:S(2)}) copy-start(f32[84]{0:T(128)} %param.25) | copy-start | bytes 1012
  60.0 1.1 %copy-start.2 = (f32[2,1,9,84,128]{4,1,3,2,0:T(1,128)S(1)}, f32[2,1,9,84,128]{4,1,3,2,0:T(1,128)}, u32[]{:S(2)}) copy-start(f32[2,1,9,84,128]{4,1,3,2,0:T(1,128)} %param.16) | copy-start | bytes 2322436
  60.0 1.2 %copy-start.27 = (f32[3,81]{1,0:T(4,128)S(1)}, f32[3,81]{1,0:T(4,128)}, u32[]{:S(2)}) copy-start(f32[3,81]{1,0:T(4,128)} %param.26) | copy-start | bytes 2920
  63.1 2.0 %copy-start.29 = (s32[128]{0:T(128)S(1)}, s32[128]{0:T(128)}, u32[]{:S(2)}) copy-start(s32[128]{0:T(128)} %param.29) | copy-start | bytes 1540
  65.7 0.6 copy-start.7
where the time goes:
time: 81.8 us; the launch traced here: 81.4 us
  Pallas kernels  32.7 us (40%)
  matrix products  26.5 us (32%)
  local copies, waits for them, and re-layouts  11.1 us (14%)
  other arithmetic  9.45 us (12%)
  between operations  1.68 us (2%)
    pallas_call x2, Pallas kernels, exchange(): pl.pallas_call(lambda *refs: exchange_kernel(count, *refs), out_shape=(ja...  20.1 us
    pallas_call x1, Pallas kernels, scatter_tiles(): pl.pallas_call(lambda *refs: scatter_kernel(offsets, group_count, curve_c...  12.6 us
    dot_general x4, matrix products, predictor(): jnp.einsum('dab,qbc->dqac', stiffness, derivative, precision=PRECISE)  7.25 us
    unnamed x88, local copies, waits for them, and re-layouts  6.33 us
    dot_general x2, matrix products, on_device(): lifted = jnp.einsum('ibt,qtic->qbc', lifting, face_flux, precision=PRECISE)  5.32 us
    add x2, other arithmetic, predictor(): integral = integral + factor * derivative  4.55 us
    dot_general x2, matrix products, on_device(): jnp.einsum('pqr,rbc->pqbc', mix, forward[time_step, 0], precision=PRECISE)  3.69 us
    dot_general x2, matrix products, turn_faces(): jnp.einsum('rts,qsic->rqtic', orientation, gathered, precision=PRECISE)  3.29 us

commit v1 on v0

--- a/solution.py
+++ b/solution.py
@@ -12,6 +12,7 @@
 
 
 PRECISE = lax.Precision.HIGHEST
+DENSE = lax.Precision.HIGH
 TIME_STEP = 0.4
 
 
@@ -35,7 +36,7 @@
     factor = TIME_STEP
     integral = factor * state
     for degree in range(1, TERMS):
-        moved = jnp.einsum("dab,qbc->dqac", stiffness, derivative, precision=PRECISE)
+        moved = jnp.einsum("dab,qbc->dqac", stiffness, derivative, precision=DENSE)
         derivative = star_sum(star_mats, moved)
         factor = factor * TIME_STEP / (degree + 1)
         integral = integral + factor * derivative
@@ -43,12 +44,12 @@
 
 
 def volume(integral, stiffness, star_mats):
-    moved = jnp.einsum("dba,qbc->dqac", stiffness, integral, precision=PRECISE)
+    moved = jnp.einsum("dba,qbc->dqac", stiffness, integral, precision=DENSE)
     return star_sum(star_mats, moved)
 
 
 def turn_faces(gathered, orientation, face_turn):
-    turned = jnp.einsum("rts,qsic->rqtic", orientation, gathered, precision=PRECISE)
+    turned = jnp.einsum("rts,qsic->rqtic", orientation, gathered, precision=DENSE)
     result = jnp.zeros_like(gathered)
     for turn_index in range(3):
         result = result + jnp.where(face_turn[None, None] == turn_index, turned[turn_index], 0.0)
@@ -201,7 +202,7 @@
     density_sum = jnp.zeros((3, cells), f32)
     for time_step in range(STEPS):
         integral = predictor(state, stiffness, star_mats)
-        own_trace = jnp.einsum("itb,qbc->qtic", face_proj, integral, precision=PRECISE)
+        own_trace = jnp.einsum("itb,qbc->qtic", face_proj, integral, precision=DENSE)
         table = own_trace.reshape(rows, 4 * cells)
         outgoing = jnp.dot(table, send_oh, precision=PRECISE)
         from_prev, from_next = exchange(outgoing[:, slots:], outgoing[:, :slots])
@@ -210,10 +211,10 @@
         gathered = jnp.dot(extended, gather_oh, precision=PRECISE).reshape(9, face_basis, 4, cells)
         oriented = turn_faces(gathered, orientation, face_turn)
         face_flux = star(own_flux, own_trace) + star(far_flux, oriented)
-        lifted = jnp.einsum("ibt,qtic->qbc", lifting, face_flux, precision=PRECISE)
+        lifted = jnp.einsum("ibt,qtic->qbc", lifting, face_flux, precision=DENSE)
         state = state + volume_term - lifted
         weighted = state * mass_weights[None, :, None]
-        mixed = jnp.einsum("pqr,rbc->pqbc", mix, forward[time_step, 0], precision=PRECISE)
+        mixed = jnp.einsum("pqr,rbc->pqbc", mix, forward[time_step, 0], precision=DENSE)
         density_sum = density_sum + jnp.sum(weighted[None] * mixed, axis=(1, 2))
 
     tile = element_cell // TILE

time: 81.8 us -> 74.5 us (0.911)
  matrix products: 26.5 us -> 19.3 us
    dot_general x14, matrix products: 23.4 us -> 16.1 us  [the longest x4 5.15 us: predictor(): moved = jnp.einsum('dab,qbc->dqac', stiffness, derivative, precision=DENSE)]
where the time goes in v1:
time: 74.5 us; the launch traced here: 74 us
  Pallas kernels  32.7 us (44%)
  matrix products  19.3 us (26%)
  local copies, waits for them, and re-layouts  11 us (15%)
  other arithmetic  9.45 us (13%)
  between operations  1.67 us (2%)
    pallas_call x2, Pallas kernels, exchange(): pl.pallas_call(lambda *refs: exchange_kernel(count, *refs), out_shape=(ja...  20.1 us
    pallas_call x1, Pallas kernels, scatter_tiles(): pl.pallas_call(lambda *refs: scatter_kernel(offsets, group_count, curve_c...  12.6 us
    unnamed x88, local copies, waits for them, and re-layouts  6.33 us
    dot_general x4, matrix products, predictor(): moved = jnp.einsum('dab,qbc->dqac', stiffness, derivative, precision=DENSE)  5.15 us
    dot_general x2, matrix products, on_device(): lifted = jnp.einsum('ibt,qtic->qbc', lifting, face_flux, precision=DENSE)  4.73 us
    add x2, other arithmetic, predictor(): integral = integral + factor * derivative  4.55 us
    dot_general x2, matrix products, on_device(): jnp.einsum('pqr,rbc->pqbc', mix, forward[time_step, 0], precision=DENSE)  2.29 us
    dot_general x2, matrix products, on_device(): jnp.dot(extended, gather_oh, precision=PRECISE)  1.86 us

profile of v1, /device:TPU:1, one launch (start us, length us, event | category | flops | bytes accessed | tf_op | source)
XLA Modules:
  0.0 74.0 jit_solution(16579808876136280716)
XLA Ops:
  0.7 0.9 %fusion.215 = (f32[1,81,128]{2,1,0:T(8,128)S(1)}, f32[1,81,128]{2,1,0:T(8,128)S(1)}, f32[1,81,128]{2,1,0:T(8,128)S(1)}) fusion(f32[3,81,128]{2,1,0:T(8,128)} %param.17), kind=kLoop, calls=%fused_computation.540 | loop fusion | bytes 248832 | tf_op jit(solution)/shard_map/slice | solution.py:28
  1.9 0.7 convolution_bitcast_fusion.7
  2.6 0.1 slice_bitcast_fusion.203
  2.7 1.8 %convolution_bitcast_fusion.6 = f32[3,9,84,128]{3,2,0,1:T(8,128)S(1)} fusion(f32[3,84,84]{2,1,0:T(8,128)S(1)} %copy-done, f32[84,128]{1,0:T(8,128)S(1)} %get-tuple-element.152, f32[9,128]{1,0:T(8,128)S(1)} %get-tuple-element.276, f32[84,128]{1,0:T(8,128)S(1)} %get-tuple-element.153, f32[9,128]{1,0:T(8,128)S(1)} %get-tuple-element.277, ...), kind=kOutput, calls=%fused_computation.11 | convolution fusion | flops 151441920 | bytes 2531520 | tf_op jit(solution)/shard_map/dab,qbc->dqac/dot_general | solution.py:39
  4.5 0.1 slice_bitcast_fusion.176
  4.6 2.3 %fusion.105 = f32[9,84,128,1]{2,1,3,0:T(8,128)S(1)} fusion(f32[1,9,84,128]{3,0,2,1:T(1,128)S(1)} %copy-done.1, f32[84,128]{1,0:T(8,128)S(1)} %get-tuple-element.125, f32[84,128]{1,0:T(8,128)S(1)} %get-tuple-element.126, f32[84,128]{1,0:T(8,128)S(1)} %get-tuple-element.127, f32[84,128]{1,0:T(8,128)S(1)} %get-tuple-element.128, ...), kind=kLoop, calls=%fused_computation.132 | loop fusion | flops 10741248 | bytes 3220992 | tf_op jit(solution)/shard_map/add | solution.py:42
  6.9 0.1 copy.126
  7.0 0.4 convolution_bitcast_fusion.9
  7.4 0.3 copy.127
  7.8 0.1 pad.8
  7.9 0.5 copy-done.28
  8.5 0.4 fusion.101
  8.9 0.7 fusion.214
  9.6 11.5 %shard_map.158 = (f32[252,128]{1,0:T(8,128)}, f32[252,128]{1,0:T(8,128)}) custom-call(f32[252,128]{1,0:T(8,128)} %get-tuple-element.219.refs_0_, f32[252,128]{1,0:T(8,128)} %get-tuple-element.218.refs_1_), custom_call_target="tpu_custom_call" | custom-call | tf_op jit(solution)/shard_map/pallas_call | solution.py:95
  21.2 0.9 %broadcast_select_fusion.2 = f32[252,128]{1,0:T(8,128)S(1)} fusion(f32[252,128]{1,0:T(8,128)} %get-tuple-element.7, pred[]{:T(512)S(6)} %eq.74), kind=kLoop, calls=%fused_computation.267 | loop fusion | flops 32256 | bytes 258049 | tf_op jit(solution)/shard_map/jit(_where)/select_n | solution.py:104
  22.1 0.9 %broadcast_select_fusion.3 = f32[252,128]{1,0:T(8,128)S(1)} fusion(f32[252,128]{1,0:T(8,128)} %get-tuple-element.6, pred[]{:T(512)S(6)} %eq.70), kind=kLoop, calls=%fused_computation.268 | loop fusion | flops 32256 | bytes 258049 | tf_op jit(solution)/shard_map/jit(_where)/select_n | solution.py:103
  23.0 0.9 %fusion.1 = f32[252,512]{1,0:T(8,128)S(1)} fusion(f32[252,128]{1,0:T(8,128)S(1)} %broadcast_select_fusion.2, f32[252,128]{1,0:T(8,128)S(1)} %broadcast_select_fusion.3, f32[252,512]{1,0:T(8,128)S(1)} %bitcast.737, s32[512]{0:T(512)S(1)} %bitcast.765), kind=kOutput, calls=%fused_computation.4 | convolution fusion | flops 1189865472 | bytes 1292288 | tf_op jit(solution)/shard_map/dot_general | solution.py:211
  24.0 0.2 reshape.394
  24.2 0.8 %convolution_bitcast_fusion.1 = f32[3,9,28,4,128]{4,2,0,3,1:T(8,128)S(1)} fusion(f32[9,28,4,128,1]{3,2,1,0,4:T(4,128)S(1)} %bitcast.735, f32[3,28,28]{2,1,0:T(8,128)S(1)} %copy-done.3), kind=kOutput, calls=%fused_computation.6 | convolution fusion | flops 65028096 | bytes 2073792 | tf_op jit(solution)/shard_map/rts,qsic->rqtic/dot_general | solution.py:52
  25.1 0.2 fusion.23
  25.4 0.3 copy-done.20
  25.6 0.0 copy-done.24
  25.7 0.7 convolution_bitcast_fusion.5
  26.4 0.1 slice_bitcast_fusion.149
  26.6 0.8 %copy-done.4 = f32[4,81,128]{2,0,1:T(4,128)S(1)} copy-done((f32[4,81,128]{2,0,1:T(4,128)S(1)}, f32[4,81,128]{2,0,1:T(4,128)}, u32[]{:S(2)}) %copy-start.4) | copy-done | bytes 165912
  27.4 0.1 copy-done.5
  27.5 0.1 slice_bitcast_fusion.212
  27.6 2.4 %fusion.2 = f32[9,84,128]{2,1,0:T(8,128)S(1)} fusion(f32[1,9,84,128]{3,0,2,1:T(1,128)S(1)} %copy-done.1, f32[28,4,128]{2,0,1:T(8,128)S(1)} %get-tuple-element.208, f32[9,4,128]{2,1,0:T(4,128)S(1)} %get-tuple-element.230, f32[28,4,128]{2,0,1:T(8,128)S(1)} %get-tuple-element.209, f32[9,4,128]{2,1,0:T(4,128)S(1)} %get-tuple-element.231, ...), kind=kOutput, calls=%fused_computation.17 | convolution fusion | flops 74866176 | bytes 3461376 | tf_op jit(solution)/shard_map/ibt,qtic->qbc/dot_general | solution.py:214
  30.0 0.9 %convolution_bitcast_fusion.4 = f32[3,9,84,128]{3,2,0,1:T(8,128)S(1)} fusion(f32[9,84,128]{2,1,0:T(8,128)S(1)} %fusion.2, f32[3,84,84]{2,1,0:T(8,128)S(1)} %copy-done), kind=kOutput, calls=%fused_computation.9 | convolution fusion | flops 146313216 | bytes 1632960 | tf_op jit(solution)/shard_map/dab,qbc->dqac/dot_general | solution.py:39
  30.9 0.1 slice_bitcast_fusion.122
  31.0 1.8 %convolution_bitcast_fusion.3 = f32[3,9,84,128]{3,2,0,1:T(8,128)S(1)} fusion(f32[3,84,84]{2,1,0:T(8,128)S(1)} %copy-done, f32[84,128]{1,0:T(8,128)S(1)} %get-tuple-element.71, f32[84,128]{1,0:T(8,128)S(1)} %get-tuple-element.72, f32[84,128]{1,0:T(8,128)S(1)} %get-tuple-element.73, f32[84,128]{1,0:T(8,128)S(1)} %get-tuple-element.74, ...), kind=kOutput, calls=%fused_computation.8 | convolution fusion | flops 151441920 | bytes 2531520 | tf_op jit(solution)/shard_map/dab,qbc->dqac/dot_general | solution.py:39
  32.8 0.1 slice_bitcast_fusion.95
  32.9 2.3 %multiply_add_fusion = f32[9,84,128]{2,1,0:T(8,128)S(1)} fusion(f32[9,84,128]{2,1,0:T(8,128)S(1)} %fusion.2, f32[84,128]{1,0:T(8,128)S(1)} %get-tuple-element.44, f32[84,128]{1,0:T(8,128)S(1)} %get-tuple-element.45, f32[84,128]{1,0:T(8,128)S(1)} %get-tuple-element.46, f32[84,128]{1,0:T(8,128)S(1)} %get-tuple-element.47, ...), kind=kLoop, calls=%fused_computation.138 | loop fusion | flops 10741248 | bytes 3220992 | tf_op jit(solution)/shard_map/add | solution.py:42
  35.2 0.4 convolution_bitcast_fusion.8
  35.6 0.3 copy.133
  35.9 0.1 pad.9
  36.1 0.4 fusion.100
  36.6 0.7 fusion.213
  37.3 8.5 %shard_map.159 = (f32[252,128]{1,0:T(8,128)}, f32[252,128]{1,0:T(8,128)}) custom-call(f32[252,128]{1,0:T(8,128)} %get-tuple-element.217.refs_0_, f32[252,128]{1,0:T(8,128)} %get-tuple-element.216.refs_1_), custom_call_target="tpu_custom_call" | custom-call | tf_op jit(solution)/shard_map/pallas_call | solution.py:95
  45.8 0.9 %broadcast_select_fusion.1 = f32[252,128]{1,0:T(8,128)S(1)} fusion(f32[252,128]{1,0:T(8,128)} %get-tuple-element.8, pred[]{:T(512)S(6)} %eq.70), kind=kLoop, calls=%fused_computation.266 | loop fusion | flops 32256 | bytes 258049 | tf_op jit(solution)/shard_map/jit(_where)/select_n | solution.py:103
  46.7 0.9 %broadcast_select_fusion = f32[252,128]{1,0:T(8,128)S(1)} fusion(f32[252,128]{1,0:T(8,128)} %get-tuple-element.9, pred[]{:T(512)S(6)} %eq.74), kind=kLoop, calls=%fused_computation.265 | loop fusion | flops 32256 | bytes 258049 | tf_op jit(solution)/shard_map/jit(_where)/select_n | solution.py:104
  47.7 0.9 %fusion = f32[252,512]{1,0:T(8,128)S(1)} fusion(f32[252,128]{1,0:T(8,128)S(1)} %broadcast_select_fusion, f32[252,128]{1,0:T(8,128)S(1)} %broadcast_select_fusion.1, f32[252,512]{1,0:T(8,128)S(1)} %bitcast.739, s32[512]{0:T(512)S(1)} %bitcast.766), kind=kOutput, calls=%fused_computation.3 | convolution fusion | flops 1189865472 | bytes 1292288 | tf_op jit(solution)/shard_map/dot_general | solution.py:211
  48.6 0.2 reshape.396
  48.8 0.8 %convolution_bitcast_fusion = f32[3,9,28,4,128]{4,2,3,1,0:T(8,128)S(1)} fusion(f32[9,28,4,128]{3,2,1,0:T(4,128)S(1)} %reshape.396, f32[3,28,28]{2,1,0:T(8,128)S(1)} %copy-done.3), kind=kOutput, calls=%fused_computation.5 | convolution fusion | flops 65028096 | bytes 2073792 | tf_op jit(solution)/shard_map/rts,qsic->rqtic/dot_general | solution.py:52
  49.7 0.2 fusion.18
  49.9 0.7 %convolution_bitcast_fusion.2 = f32[3,9,84,128]{3,2,0,1:T(8,128)S(1)} fusion(f32[9,84,128]{2,1,0:T(8,128)S(1)} %multiply_add_fusion, f32[3,84,84]{2,1,0:T(8,128)S(1)} %copy-done), kind=kOutput, calls=%fused_computation.7 | convolution fusion | flops 146313216 | bytes 1632960 | tf_op jit(solution)/shard_map/dba,qbc->dqac/dot_general | solution.py:47
  50.7 0.1 slice_bitcast_fusion.68
  50.9 0.6 copy-done.9
  51.5 0.0 copy-done.15
  51.6 0.1 copy-done.31
  51.7 2.4 %broadcast_multiply_fusion = (f32[9,84,128]{2,1,0:T(8,128)S(1)}, f32[9,84,128]{2,1,0:T(8,128)S(1)}, f32[9,84,128]{2,1,0:T(8,128)S(1)}) fusion(f32[84]{0:T(128)S(1)} %copy-done.34, f32[9,84,128]{2,1,0:T(8,128)S(1)} %fusion.2, f32[4,84,28]{1,0,2:T(4,128)S(1)} %copy-done.31, f32[28,4,128]{2,0,1:T(8,128)S(1)} %get-tuple-element.190, ...), kind=kOutput, calls=%fused_computation.217 | convolution fusion | flops 75059712 | bytes 4235856 | tf_op jit(solution)/shard_map/ibt,qtic->qbc/dot_general | solution.py:214
  54.1 0.1 copy.140
  54.2 1.0 %copy-done.2 = f32[2,1,9,84,128]{4,1,3,2,0:T(1,128)S(1)} copy-done((f32[2,1,9,84,128]{4,1,3,2,0:T(1,128)S(1)}, f32[2,1,9,84,128]{4,1,3,2,0:T(1,128)}, u32[]{:S(2)}) %copy-start.2) | copy-done | bytes 774168
  55.2 0.1 fusion.212
  55.3 0.1 reshape.417
  55.3 1.3 %multiply_reduce_fusion = f32[3,128]{1,0:T(4,128)S(1)} fusion(f32[9,84,128]{2,0,1:T(8,128)S(1)} %copy.140, f32[1,1,9,84,128]{4,1,3,2,0:T(1,128)S(1)} %get-tuple-element.178, f32[3,9,9,1]{2,1,0,3:T(8,128)S(1)} %reshape.417), kind=kOutput, calls=%fused_computation | convolution fusion | flops 16256640 | bytes 776652 | tf_op jit(solution)/shard_map/pqr,rbc->pqbc/dot_general | solution.py:217
  56.6 0.1 copy.137
  56.7 1.0 %multiply_reduce_fusion.1 = f32[3,128]{1,0:T(4,128)S(1)} fusion(f32[9,84,128]{2,0,1:T(8,128)S(1)} %copy.137, f32[1,1,9,84,128]{4,1,3,2,0:T(1,128)S(1)} %get-tuple-element.179, f32[3,9,9,1]{2,1,0,3:T(8,128)S(1)} %reshape.417), kind=kOutput, calls=%fused_computation.1 | convolution fusion | flops 16256640 | bytes 776652 | tf_op jit(solution)/shard_map/pqr,rbc->pqbc/dot_general | solution.py:217
  57.8 0.4 fusion.16
  58.4 0.6 copy-done.7
  59.0 12.6 %shard_map.160 = f32[11,3,128]{2,1,0:T(4,128)} custom-call(f32[11,3,128]{2,1,0:T(4,128)} %copy-done.7), custom_call_target="tpu_custom_call" | custom-call | tf_op jit(solution)/shard_map/pallas_call | solution.py:147
  71.6 0.8 %reduce_sum.31 = f32[3,128]{1,0:T(4,128)S(1)} reduce(f32[11,3,128]{2,1,0:T(4,128)} %shard_map.160, f32[]{:T(128)} %constant.77.clone.1), dimensions={0}, to_apply=%region_2.3 | reduce | flops 3840 | bytes 18436 | tf_op jit(solution)/shard_map/reduce_sum | solution.py:158
  72.3 0.6 copy.144
  72.9 1.1 %copy.143 = f32[1,9,84,128]{3,0,2,1:T(1,128)} copy(f32[1,9,84,128]{3,2,1,0:T(8,128)S(1)} %bitcast.744) | data formatting | bytes 774144
  (109 shorter events, 0.9 us)
Async XLA Ops:
  0.6 1.2 %copy-start = (f32[3,84,84]{2,1,0:T(8,128)S(1)}, f32[3,84,84]{2,1,0:T(8,128)}, u32[]{:S(2)}) copy-start(f32[3,84,84]{2,1,0:T(8,128)} %param.20) | copy-start | bytes 254020
  0.6 1.2 %copy-start.1 = (f32[1,9,84,128]{3,0,2,1:T(1,128)S(1)}, f32[1,9,84,128]{3,0,2,1:T(1,128)}, u32[]{:S(2)}) copy-start(f32[1,9,84,128]{3,0,2,1:T(1,128)} %param.15) | copy-start | bytes 1161220
  4.6 2.3 %copy-start.6 = (f32[112,84]{0,1:T(8,128)S(1)}, f32[112,84]{0,1:T(8,128)}, u32[]{:S(2)}) copy-start(f32[112,84]{0,1:T(8,128)} %param.21) | copy-start | bytes 112900
  7.8 0.7 copy-start.28
  7.9 15.1 %copy-start.32 = (s32[4,128]{1,0:T(4,128)S(1)}, s32[4,128]{1,0:T(4,128)}, u32[]{:S(2)}) copy-start(s32[4,128]{1,0:T(4,128)} %param.27) | copy-start | bytes 6148
  23.0 1.2 %copy-start.3 = (f32[3,28,28]{2,1,0:T(8,128)S(1)}, f32[3,28,28]{2,1,0:T(8,128)}, u32[]{:S(2)}) copy-start(f32[3,28,28]{2,1,0:T(8,128)} %param.23) | copy-start | bytes 28228
  24.2 0.9 %copy-start.26 = (s32[4,128]{1,0:T(4,128)S(1)}, s32[4,128]{1,0:T(4,128)}, u32[]{:S(2)}) copy-start(s32[4,128]{1,0:T(4,128)} %param.24) | copy-start | bytes 6148
  25.1 0.6 copy-start.20
  25.1 0.6 copy-start.22
  25.1 0.6 copy-start.24
  26.5 0.9 %copy-start.4 = (f32[4,81,128]{2,0,1:T(4,128)S(1)}, f32[4,81,128]{2,0,1:T(4,128)}, u32[]{:S(2)}) copy-start(f32[4,81,128]{2,0,1:T(4,128)} %param.19) | copy-start | bytes 497668
  26.5 1.0 %copy-start.5 = (f32[4,81,128]{2,0,1:T(4,128)S(1)}, f32[4,81,128]{2,0,1:T(4,128)}, u32[]{:S(2)}) copy-start(f32[4,81,128]{2,0,1:T(4,128)} %param.18) | copy-start | bytes 497668
  26.5 1.1 %copy-start.30 = (f32[4,84,28]{1,0,2:T(4,128)S(1)}, f32[4,84,28]{1,0,2:T(4,128)}, u32[]{:S(2)}) copy-start(f32[4,84,28]{1,0,2:T(4,128)} %param.22) | copy-start | bytes 112900
  27.5 2.4 %copy-start.8 = (f32[9,4,128]{2,1,0:T(4,128)}, f32[9,4,128]{2,1,0:T(4,128)S(1)}, u32[]{:S(2)}) copy-start(f32[9,4,128]{2,1,0:T(4,128)S(1)} %get-tuple-element.305) | copy-start | bytes 55300
  27.5 2.4 %copy-start.10 = (f32[9,4,128]{2,1,0:T(4,128)}, f32[9,4,128]{2,1,0:T(4,128)S(1)}, u32[]{:S(2)}) copy-start(f32[9,4,128]{2,1,0:T(4,128)S(1)} %get-tuple-element.306) | copy-start | bytes 55300
  27.6 2.4 %copy-start.12 = (f32[9,4,128]{2,1,0:T(4,128)}, f32[9,4,128]{2,1,0:T(4,128)S(1)}, u32[]{:S(2)}) copy-start(f32[9,4,128]{2,1,0:T(4,128)S(1)} %get-tuple-element.307) | copy-start | bytes 55300
  27.6 2.4 %copy-start.14 = (f32[9,4,128]{2,1,0:T(4,128)}, f32[9,4,128]{2,1,0:T(4,128)S(1)}, u32[]{:S(2)}) copy-start(f32[9,4,128]{2,1,0:T(4,128)S(1)} %get-tuple-element.308) | copy-start | bytes 55300
  27.6 2.4 %copy-start.16 = (f32[9,4,128]{2,1,0:T(4,128)}, f32[9,4,128]{2,1,0:T(4,128)S(1)}, u32[]{:S(2)}) copy-start(f32[9,4,128]{2,1,0:T(4,128)S(1)} %get-tuple-element.309) | copy-start | bytes 55300
  27.6 2.4 %copy-start.18 = (f32[9,4,128]{2,1,0:T(4,128)}, f32[9,4,128]{2,1,0:T(4,128)S(1)}, u32[]{:S(2)}) copy-start(f32[9,4,128]{2,1,0:T(4,128)S(1)} %get-tuple-element.310) | copy-start | bytes 55300
  36.1 11.6 %copy-start.33 = (s32[4,128]{1,0:T(4,128)S(1)}, s32[4,128]{1,0:T(4,128)}, u32[]{:S(2)}) copy-start(s32[4,128]{1,0:T(4,128)} %param.27) | copy-start | bytes 6148
  48.8 0.9 %copy-start.21 = (pred[4,128]{1,0:T(4,128)(4,1)S(1)}, pred[4,128]{1,0:T(4,128)(4,1)}, u32[]{:S(2)}) copy-start(pred[4,128]{1,0:T(4,128)(4,1)} %copy-done.20) | copy-start | bytes 1540
  48.8 0.9 %copy-start.23 = (pred[4,128]{1,0:T(4,128)(4,1)S(1)}, pred[4,128]{1,0:T(4,128)(4,1)}, u32[]{:S(2)}) copy-start(pred[4,128]{1,0:T(4,128)(4,1)} %copy-done.22) | copy-start | bytes 1540
  48.8 0.9 %copy-start.25 = (pred[4,128]{1,0:T(4,128)(4,1)S(1)}, pred[4,128]{1,0:T(4,128)(4,1)}, u32[]{:S(2)}) copy-start(pred[4,128]{1,0:T(4,128)(4,1)} %copy-done.24) | copy-start | bytes 1540
  50.8 0.7 copy-start.9
  50.8 0.7 copy-start.11
  50.8 0.7 copy-start.13
  50.8 0.7 %copy-start.15 = (f32[9,4,128]{2,1,0:T(4,128)S(1)}, f32[9,4,128]{2,1,0:T(4,128)}, u32[]{:S(2)}) copy-start(f32[9,4,128]{2,1,0:T(4,128)} %copy-done.14) | copy-start | bytes 55300
  50.8 0.8 %copy-start.17 = (f32[9,4,128]{2,1,0:T(4,128)S(1)}, f32[9,4,128]{2,1,0:T(4,128)}, u32[]{:S(2)}) copy-start(f32[9,4,128]{2,1,0:T(4,128)} %copy-done.16) | copy-start | bytes 55300
  50.8 0.8 %copy-start.19 = (f32[9,4,128]{2,1,0:T(4,128)S(1)}, f32[9,4,128]{2,1,0:T(4,128)}, u32[]{:S(2)}) copy-start(f32[9,4,128]{2,1,0:T(4,128)} %copy-done.18) | copy-start | bytes 55300
  50.8 0.9 %copy-start.31 = (f32[4,84,28]{1,0,2:T(4,128)S(1)}, f32[4,84,28]{1,0,2:T(4,128)}, u32[]{:S(2)}) copy-start(f32[4,84,28]{1,0,2:T(4,128)} %param.22) | copy-start | bytes 112900
  50.8 0.9 %copy-start.34 = (f32[84]{0:T(128)S(1)}, f32[84]{0:T(128)}, u32[]{:S(2)}) copy-start(f32[84]{0:T(128)} %param.25) | copy-start | bytes 1012
  54.1 1.1 %copy-start.2 = (f32[2,1,9,84,128]{4,1,3,2,0:T(1,128)S(1)}, f32[2,1,9,84,128]{4,1,3,2,0:T(1,128)}, u32[]{:S(2)}) copy-start(f32[2,1,9,84,128]{4,1,3,2,0:T(1,128)} %param.16) | copy-start | bytes 2322436
  54.1 1.2 %copy-start.27 = (f32[3,81]{1,0:T(4,128)S(1)}, f32[3,81]{1,0:T(4,128)}, u32[]{:S(2)}) copy-start(f32[3,81]{1,0:T(4,128)} %param.26) | copy-start | bytes 2920
  56.6 1.2 %copy-start.29 = (s32[128]{0:T(128)S(1)}, s32[128]{0:T(128)}, u32[]{:S(2)}) copy-start(s32[128]{0:T(128)} %param.29) | copy-start | bytes 1540
  58.3 0.6 copy-start.7

commit v2 on v1

--- a/solution.py
+++ b/solution.py
@@ -56,13 +56,30 @@
     return result
 
 
-def exchange_kernel(count, to_next, to_prev, from_prev, from_next, send_sem, recv_sem):
+def add_volume(integral, stiff_t, mats, volume_out, axis_dirs):
+    for axis_dir in axis_dirs:
+        for source in range(9):
+            moved = jnp.dot(
+                stiff_t[axis_dir], integral[source], precision=PRECISE, preferred_element_type=jnp.float32
+            )
+            for target in range(9):
+                term = mats[axis_dir, pl.ds(9 * target + source, 1), :] * moved
+                if axis_dir == 0 and source == 0:
+                    volume_out[target] = term
+                else:
+                    volume_out[target] = volume_out[target] + term
+
+
+def exchange_kernel(
+    count, to_next, to_prev, integral, stiff_t, mats, from_prev, from_next, volume_out, send_sem, recv_sem
+):
     group = lax.axis_index("grp")
     me = lax.axis_index("curve")
     right, left = lax.rem(me + 1, count), lax.rem(me + count - 1, count)
     barrier = pltpu.get_barrier_semaphore()
     for side in (left, right):
         pl.semaphore_signal(barrier, inc=1, device_id=(group, side), device_id_type=pl.DeviceIdType.MESH)
+    add_volume(integral, stiff_t, mats, volume_out, (0,))
     pl.semaphore_wait(barrier, 2)
     copies = [
         pltpu.make_async_remote_copy(
@@ -84,25 +101,30 @@
     ]
     for copy in copies:
         copy.start()
+    add_volume(integral, stiff_t, mats, volume_out, (1, 2))
     for copy in copies:
         copy.wait()
 
 
-def exchange(to_next, to_prev):
+def exchange(to_next, to_prev, integral, stiff_t, star_mats):
     count = lax.axis_size("curve")
     me = lax.axis_index("curve")
     vmem = pl.BlockSpec(memory_space=pltpu.VMEM)
-    from_prev, from_next = pl.pallas_call(
+    from_prev, from_next, volume_term = pl.pallas_call(
         lambda *refs: exchange_kernel(count, *refs),
-        out_shape=(jax.ShapeDtypeStruct(to_next.shape, to_next.dtype),) * 2,
-        in_specs=[vmem, vmem],
-        out_specs=(vmem, vmem),
+        out_shape=(
+            jax.ShapeDtypeStruct(to_next.shape, to_next.dtype),
+            jax.ShapeDtypeStruct(to_next.shape, to_next.dtype),
+            jax.ShapeDtypeStruct(integral.shape, integral.dtype),
+        ),
+        in_specs=[vmem] * 5,
+        out_specs=(vmem, vmem, vmem),
         scratch_shapes=[pltpu.SemaphoreType.DMA((2,)), pltpu.SemaphoreType.DMA((2,))],
         compiler_params=pltpu.CompilerParams(collective_id=0, has_side_effects=True),
-    )(to_next, to_prev)
+    )(to_next, to_prev, integral, stiff_t, star_mats)
     from_prev = jnp.where(me == 0, 0.0, from_prev)
     from_next = jnp.where(me == count - 1, 0.0, from_next)
-    return from_prev, from_next
+    return from_prev, from_next, volume_term
 
 
 def scatter_kernel(offsets, group_count, curve_count, chunks, received, send_sem, recv_sem):
@@ -196,6 +218,7 @@
     gather_oh = (table_cols[:, None] == neighbour.reshape(-1)[None, :]).astype(f32)
 
     mix = param_mixing.reshape(3, 9, 9)
+    stiff_t = jnp.transpose(stiffness, (0, 2, 1))
     state = with_layout_constraint(
         adjoint.reshape(adjoint.shape[1:]), Layout((0, 1, 2))
     )
@@ -205,8 +228,9 @@
         own_trace = jnp.einsum("itb,qbc->qtic", face_proj, integral, precision=DENSE)
         table = own_trace.reshape(rows, 4 * cells)
         outgoing = jnp.dot(table, send_oh, precision=PRECISE)
-        from_prev, from_next = exchange(outgoing[:, slots:], outgoing[:, :slots])
-        volume_term = volume(integral, stiffness, star_mats)
+        from_prev, from_next, volume_term = exchange(
+            outgoing[:, slots:], outgoing[:, :slots], integral, stiff_t, star_mats
+        )
         extended = jnp.concatenate([table, from_prev, from_next], axis=1)
         gathered = jnp.dot(extended, gather_oh, precision=PRECISE).reshape(9, face_basis, 4, cells)
         oriented = turn_faces(gathered, orientation, face_turn)

time: 74.5 us -> 73.2 us (0.983)
  matrix products: 19.3 us -> 16.5 us
  local copies, waits for them, and re-layouts: 11 us -> 11.9 us
  Pallas kernels: 32.7 us -> 33.5 us
    dot_general x2, matrix products: 4.73 us -> 2.96 us  [on_device(): lifted = jnp.einsum('ibt,qtic->qbc', lifting, face_flux, precision=DENSE)]
    dot_general x2 -> x0, matrix products: 1.48 us -> none  [volume(): moved = jnp.einsum('dba,qbc->dqac', stiffness, integral, precision=DENSE)]
    unnamed x88 -> x57, local copies, waits for them, and re-layouts: 6.33 us -> 7.39 us
    pallas_call x2, Pallas kernels: 20.1 us -> 20.9 us  [exchange(): pl.pallas_call(lambda *refs: exchange_kernel(count, *refs), out_shape=(ja...]
where the time goes in v2:
time: 73.2 us; the launch traced here: 72.8 us
  Pallas kernels  33.5 us (46%)
  matrix products  16.5 us (23%)
  local copies, waits for them, and re-layouts  11.9 us (16%)
  other arithmetic  9.47 us (13%)
  between operations  1.42 us (2%)
    pallas_call x2, Pallas kernels, exchange(): pl.pallas_call(lambda *refs: exchange_kernel(count, *refs), out_shape=(ja...  20.9 us
    pallas_call x1, Pallas kernels, scatter_tiles(): pl.pallas_call(lambda *refs: scatter_kernel(offsets, group_count, curve_c...  12.6 us
    unnamed x57, local copies, waits for them, and re-layouts  7.39 us
    dot_general x4, matrix products, predictor(): moved = jnp.einsum('dab,qbc->dqac', stiffness, derivative, precision=DENSE)  5.83 us
    add x2, other arithmetic, predictor(): integral = integral + factor * derivative  4.56 us
    dot_general x2, matrix products, on_device(): lifted = jnp.einsum('ibt,qtic->qbc', lifting, face_flux, precision=DENSE)  2.96 us
    dot_general x2, matrix products, on_device(): jnp.einsum('pqr,rbc->pqbc', mix, forward[time_step, 0], precision=DENSE)  2.05 us
    dot_general x2, matrix products, on_device(): jnp.dot(extended, gather_oh, precision=PRECISE)  1.86 us

profile of v2, /device:TPU:1, one launch (start us, length us, event | category | flops | bytes accessed | tf_op | source)
XLA Modules:
  0.0 72.8 jit_solution(4413515645229658624)
XLA Ops:
  0.6 0.0 copy-start
  0.7 0.9 %fusion.212 = (f32[1,81,128]{2,1,0:T(8,128)S(1)}, f32[1,81,128]{2,1,0:T(8,128)S(1)}, f32[1,81,128]{2,1,0:T(8,128)S(1)}) fusion(f32[3,81,128]{2,1,0:T(8,128)} %refs_4_.3), kind=kLoop, calls=%fused_computation.481 | loop fusion | bytes 248832 | tf_op jit(solution)/shard_map/slice | solution.py:28
  1.9 1.6 %convolution_bitcast_fusion.5 = f32[3,9,84,128]{3,2,0,1:T(8,128)S(1)} fusion(f32[1,9,84,128]{3,0,2,1:T(1,128)S(1)} %copy-done.3, f32[3,84,84]{2,1,0:T(8,128)} %param.20), kind=kOutput, calls=%fused_computation.10 | convolution fusion | flops 146313216 | bytes 1632960 | tf_op jit(solution)/shard_map/dab,qbc->dqac/dot_general | solution.py:39
  3.5 0.1 slice_bitcast_fusion.149
  3.6 0.8 %copy-done.4 = f32[3,84,84]{2,1,0:T(8,128)S(1)} copy-done((f32[3,84,84]{2,1,0:T(8,128)S(1)}, f32[3,84,84]{2,1,0:T(8,128)}, u32[]{:S(2)}) %copy-start.4) | copy-done | bytes 84696
  4.4 1.8 %convolution_bitcast_fusion.4 = f32[3,9,84,128]{3,2,0,1:T(8,128)S(1)} fusion(f32[3,84,84]{2,1,0:T(8,128)S(1)} %copy-done.4, f32[84,128]{1,0:T(8,128)S(1)} %get-tuple-element.102, f32[9,128]{1,0:T(8,128)S(1)} %get-tuple-element.226, f32[84,128]{1,0:T(8,128)S(1)} %get-tuple-element.103, f32[9,128]{1,0:T(8,128)S(1)} %get-tuple-element.227, ...), kind=kOutput, calls=%fused_computation.9 | convolution fusion | flops 151441920 | bytes 2531520 | tf_op jit(solution)/shard_map/dab,qbc->dqac/dot_general | solution.py:39
  6.1 0.1 slice_bitcast_fusion.122
  6.3 2.3 %fusion.104.refs_2_ = f32[9,84,128]{2,1,0:T(8,128)S(1)} fusion(f32[1,9,84,128]{3,0,2,1:T(1,128)S(1)} %copy-done.3, f32[84,128]{1,0:T(8,128)S(1)} %get-tuple-element.75, f32[84,128]{1,0:T(8,128)S(1)} %get-tuple-element.76, f32[84,128]{1,0:T(8,128)S(1)} %get-tuple-element.77, f32[84,128]{1,0:T(8,128)S(1)} %get-tuple-element.78, ...), kind=kLoop, calls=%fused_computation.129 | loop fusion | flops 10741248 | bytes 3220992 | tf_op jit(solution)/shard_map/add | solution.py:42
  8.6 0.1 copy.123
  8.7 0.4 convolution_bitcast_fusion.7
  9.1 0.0 copy-start.12
  9.1 0.3 copy.124
  9.4 0.1 pad.8
  9.6 0.0 copy-start.17
  9.6 0.2 copy-done.12
  9.8 0.4 fusion.101
  10.2 0.7 fusion.211
  10.9 0.8 %copy.125 = f32[3,84,84]{1,2,0:T(8,128)} copy(f32[3,84,84]{2,1,0:T(8,128)S(1)} %copy-done.4) | data formatting | bytes 169344 | tf_op args[5]
  11.7 11.9 %shard_map.158 = (f32[252,128]{1,0:T(8,128)}, f32[252,128]{1,0:T(8,128)}, f32[9,84,128]{2,1,0:T(8,128)}) custom-call(f32[252,128]{1,0:T(8,128)} %get-tuple-element.169.refs_0_, f32[252,128]{1,0:T(8,128)} %get-tuple-element.168.refs_1_, f32[9,84,128]{2,1,0:T(8,128)} %copy-done.1, f32[3,84,84]{2,1,0:T(8,128)} %bitcast.622, f32[3,81,128]{2,1,0:T(8,128)} %refs_4_.3), custom_call_target="tpu_custom_call" | custom-call | tf_op jit(solution)/shard_map/pallas_call | solution.py:113
  23.7 0.9 %broadcast_select_fusion.2 = f32[252,128]{1,0:T(8,128)S(1)} fusion(f32[252,128]{1,0:T(8,128)} %get-tuple-element.10, pred[]{:T(512)S(6)} %eq.74), kind=kLoop, calls=%fused_computation.262 | loop fusion | flops 32256 | bytes 258049 | tf_op jit(solution)/shard_map/jit(_where)/select_n | solution.py:126
  24.6 0.9 %broadcast_select_fusion.3 = f32[252,128]{1,0:T(8,128)S(1)} fusion(f32[252,128]{1,0:T(8,128)} %get-tuple-element.9, pred[]{:T(512)S(6)} %eq.73), kind=kLoop, calls=%fused_computation.263 | loop fusion | flops 32256 | bytes 258049 | tf_op jit(solution)/shard_map/jit(_where)/select_n | solution.py:125
  25.5 0.9 %fusion.1 = f32[252,512]{1,0:T(8,128)S(1)} fusion(f32[252,128]{1,0:T(8,128)S(1)} %broadcast_select_fusion.2, f32[252,128]{1,0:T(8,128)S(1)} %broadcast_select_fusion.3, f32[252,512]{1,0:T(8,128)S(1)} %bitcast.615, s32[512]{0:T(512)S(1)} %bitcast.643), kind=kOutput, calls=%fused_computation.4 | convolution fusion | flops 1189865472 | bytes 1292288 | tf_op jit(solution)/shard_map/dot_general | solution.py:235
  26.5 0.2 reshape.286
  26.7 0.8 %convolution_bitcast_fusion.1 = f32[3,9,28,4,128]{4,2,0,3,1:T(8,128)S(1)} fusion(f32[9,28,4,128,1]{3,2,1,0,4:T(4,128)S(1)} %bitcast.613, f32[3,28,28]{2,1,0:T(8,128)S(1)} %copy-done), kind=kOutput, calls=%fused_computation.6 | convolution fusion | flops 65028096 | bytes 2073792 | tf_op jit(solution)/shard_map/rts,qsic->rqtic/dot_general | solution.py:52
  27.6 0.2 fusion.23
  27.8 0.0 copy-start.6
  27.9 0.8 %copy-done.6 = f32[4,81,128]{2,0,1:T(4,128)S(1)} copy-done((f32[4,81,128]{2,0,1:T(4,128)S(1)}, f32[4,81,128]{2,0,1:T(4,128)}, u32[]{:S(2)}) %copy-start.6) | copy-done | bytes 165912
  28.7 0.1 copy-done.7
  28.8 0.1 slice_bitcast_fusion.158
  28.8 0.1 copy-done.14
  28.9 1.4 %fusion.2 = f32[9,84,128]{2,1,0:T(8,128)S(1)} fusion(f32[9,84,128]{2,1,0:T(8,128)S(1)} %copy-done.14, f32[1,9,84,128]{3,0,2,1:T(1,128)S(1)} %copy-done.3, f32[28,4,128]{2,0,1:T(8,128)S(1)} %get-tuple-element.158, f32[9,4,128]{2,1,0:T(4,128)S(1)} %get-tuple-element.180, f32[28,4,128]{2,0,1:T(8,128)S(1)} %get-tuple-element.159, ...), kind=kOutput, calls=%fused_computation.15 | convolution fusion | flops 69737472 | bytes 2562816 | tf_op jit(solution)/shard_map/ibt,qtic->qbc/dot_general | solution.py:238
  30.4 0.7 convolution_bitcast_fusion.3
  31.1 0.1 slice_bitcast_fusion.95
  31.2 1.8 %convolution_bitcast_fusion.2 = f32[3,9,84,128]{3,2,0,1:T(8,128)S(1)} fusion(f32[3,84,84]{2,1,0:T(8,128)S(1)} %copy-done.4, f32[84,128]{1,0:T(8,128)S(1)} %get-tuple-element.48, f32[84,128]{1,0:T(8,128)S(1)} %get-tuple-element.49, f32[84,128]{1,0:T(8,128)S(1)} %get-tuple-element.50, f32[84,128]{1,0:T(8,128)S(1)} %get-tuple-element.51, ...), kind=kOutput, calls=%fused_computation.7 | convolution fusion | flops 151441920 | bytes 2531520 | tf_op jit(solution)/shard_map/dab,qbc->dqac/dot_general | solution.py:39
  33.0 0.1 slice_bitcast_fusion.68
  33.1 2.3 %multiply_add_fusion.refs_2_ = f32[9,84,128]{2,1,0:T(8,128)S(1)} fusion(f32[9,84,128]{2,1,0:T(8,128)S(1)} %fusion.2, f32[84,128]{1,0:T(8,128)S(1)} %get-tuple-element.21, f32[84,128]{1,0:T(8,128)S(1)} %get-tuple-element.22, f32[84,128]{1,0:T(8,128)S(1)} %get-tuple-element.23, f32[84,128]{1,0:T(8,128)S(1)} %get-tuple-element.24, ...), kind=kLoop, calls=%fused_computation.135 | loop fusion | flops 10741248 | bytes 3220992 | tf_op jit(solution)/shard_map/add | solution.py:42
  35.4 0.4 convolution_bitcast_fusion.6
  35.8 0.3 copy.130
  36.2 0.1 pad.9
  36.3 0.4 fusion.100
  36.8 0.7 fusion.210
  37.5 8.9 %shard_map.159 = (f32[252,128]{1,0:T(8,128)}, f32[252,128]{1,0:T(8,128)}, f32[9,84,128]{2,1,0:T(8,128)}) custom-call(f32[252,128]{1,0:T(8,128)} %get-tuple-element.167.refs_0_, f32[252,128]{1,0:T(8,128)} %get-tuple-element.166.refs_1_, f32[9,84,128]{2,1,0:T(8,128)} %copy-done.2, f32[3,84,84]{2,1,0:T(8,128)} %bitcast.623, f32[3,81,128]{2,1,0:T(8,128)} %refs_4_.3), custom_call_target="tpu_custom_call" | custom-call | tf_op jit(solution)/shard_map/pallas_call | solution.py:113
  46.4 0.9 %broadcast_select_fusion.1 = f32[252,128]{1,0:T(8,128)S(1)} fusion(f32[252,128]{1,0:T(8,128)} %get-tuple-element.12, pred[]{:T(512)S(6)} %eq.73), kind=kLoop, calls=%fused_computation.261 | loop fusion | flops 32256 | bytes 258049 | tf_op jit(solution)/shard_map/jit(_where)/select_n | solution.py:125
  47.3 0.9 %broadcast_select_fusion = f32[252,128]{1,0:T(8,128)S(1)} fusion(f32[252,128]{1,0:T(8,128)} %get-tuple-element.13, pred[]{:T(512)S(6)} %eq.74), kind=kLoop, calls=%fused_computation.260 | loop fusion | flops 32256 | bytes 258049 | tf_op jit(solution)/shard_map/jit(_where)/select_n | solution.py:126
  48.3 0.9 %fusion = f32[252,512]{1,0:T(8,128)S(1)} fusion(f32[252,128]{1,0:T(8,128)S(1)} %broadcast_select_fusion, f32[252,128]{1,0:T(8,128)S(1)} %broadcast_select_fusion.1, f32[252,512]{1,0:T(8,128)S(1)} %bitcast.617, s32[512]{0:T(512)S(1)} %bitcast.644), kind=kOutput, calls=%fused_computation.3 | convolution fusion | flops 1189865472 | bytes 1292288 | tf_op jit(solution)/shard_map/dot_general | solution.py:235
  49.2 0.2 reshape.288
  49.4 0.8 %convolution_bitcast_fusion = f32[3,9,28,4,128]{4,2,3,1,0:T(8,128)S(1)} fusion(f32[9,28,4,128]{3,2,1,0:T(4,128)S(1)} %reshape.288, f32[3,28,28]{2,1,0:T(8,128)S(1)} %copy-done), kind=kOutput, calls=%fused_computation.5 | convolution fusion | flops 65028096 | bytes 2073792 | tf_op jit(solution)/shard_map/rts,qsic->rqtic/dot_general | solution.py:52
  50.2 0.2 fusion.18
  50.6 0.9 %copy-done.15 = f32[9,84,128]{2,1,0:T(8,128)S(1)} copy-done((f32[9,84,128]{2,1,0:T(8,128)S(1)}, f32[9,84,128]{2,1,0:T(8,128)}, u32[]{:S(2)}) %copy-start.15) | copy-done | bytes 387096
  51.4 1.5 %broadcast_multiply_fusion = (f32[9,84,128]{2,1,0:T(8,128)S(1)}, f32[9,84,128]{2,1,0:T(8,128)S(1)}, f32[9,84,128]{2,1,0:T(8,128)S(1)}) fusion(f32[84]{0:T(128)S(1)} %copy-done.18, f32[9,84,128]{2,1,0:T(8,128)S(1)} %fusion.2, f32[4,84,28]{1,0,2:T(4,128)S(1)} %copy-done.16, f32[28,4,128]{2,0,1:T(8,128)S(1)} %get-tuple-element.140, ...), kind=kOutput, calls=%fused_computation.214 | convolution fusion | flops 69931008 | bytes 3337296 | tf_op jit(solution)/shard_map/ibt,qtic->qbc/dot_general | solution.py:238
  53.0 0.0 copy-start.11
  53.0 0.1 copy.137
  53.1 1.0 %copy-done.5 = f32[2,1,9,84,128]{4,1,3,2,0:T(1,128)S(1)} copy-done((f32[2,1,9,84,128]{4,1,3,2,0:T(1,128)S(1)}, f32[2,1,9,84,128]{4,1,3,2,0:T(1,128)}, u32[]{:S(2)}) %copy-start.5) | copy-done | bytes 774168
  54.1 0.1 fusion.209
  54.2 0.1 reshape.307
  54.2 1.0 %multiply_reduce_fusion = f32[3,128]{1,0:T(4,128)S(1)} fusion(f32[9,84,128]{2,0,1:T(8,128)S(1)} %copy.137, f32[1,1,9,84,128]{4,1,3,2,0:T(1,128)S(1)} %get-tuple-element.128, f32[3,9,9,1]{2,1,0,3:T(8,128)S(1)} %reshape.307), kind=kOutput, calls=%fused_computation | convolution fusion | flops 16256640 | bytes 776652 | tf_op jit(solution)/shard_map/pqr,rbc->pqbc/dot_general | solution.py:241
  55.3 0.1 copy.134
  55.4 1.0 %multiply_reduce_fusion.1 = f32[3,128]{1,0:T(4,128)S(1)} fusion(f32[9,84,128]{2,0,1:T(8,128)S(1)} %copy.134, f32[1,1,9,84,128]{4,1,3,2,0:T(1,128)S(1)} %get-tuple-element.129, f32[3,9,9,1]{2,1,0,3:T(8,128)S(1)} %reshape.307), kind=kOutput, calls=%fused_computation.1 | convolution fusion | flops 16256640 | bytes 776652 | tf_op jit(solution)/shard_map/pqr,rbc->pqbc/dot_general | solution.py:241
  56.5 0.4 fusion.16
  57.0 0.6 copy-done.9
  57.6 12.6 %shard_map.160 = f32[11,3,128]{2,1,0:T(4,128)} custom-call(f32[11,3,128]{2,1,0:T(4,128)} %copy-done.9), custom_call_target="tpu_custom_call" | custom-call | tf_op jit(solution)/shard_map/pallas_call | solution.py:169
  70.3 0.8 %reduce_sum.31 = f32[3,128]{1,0:T(4,128)S(1)} reduce(f32[11,3,128]{2,1,0:T(4,128)} %shard_map.160, f32[]{:T(128)} %constant.77.clone.1), dimensions={0}, to_apply=%region_2.3 | reduce | flops 3840 | bytes 18436 | tf_op jit(solution)/shard_map/reduce_sum | solution.py:180
  71.0 0.6 copy.141
  71.6 1.1 %copy.140 = f32[1,9,84,128]{3,0,2,1:T(1,128)} copy(f32[1,9,84,128]{3,2,1,0:T(8,128)S(1)} %bitcast.624) | data formatting | bytes 774144
  (72 shorter events, 0.7 us)
Async XLA Ops:
  0.6 26.0 %copy-start = (f32[3,28,28]{2,1,0:T(8,128)S(1)}, f32[3,28,28]{2,1,0:T(8,128)}, u32[]{:S(2)}) copy-start(f32[3,28,28]{2,1,0:T(8,128)} %param.23) | copy-start | bytes 28228
  0.6 1.2 %copy-start.3 = (f32[1,9,84,128]{3,0,2,1:T(1,128)S(1)}, f32[1,9,84,128]{3,0,2,1:T(1,128)}, u32[]{:S(2)}) copy-start(f32[1,9,84,128]{3,0,2,1:T(1,128)} %param.15) | copy-start | bytes 1161220
  3.5 0.9 %copy-start.4 = (f32[3,84,84]{2,1,0:T(8,128)S(1)}, f32[3,84,84]{2,1,0:T(8,128)}, u32[]{:S(2)}) copy-start(f32[3,84,84]{2,1,0:T(8,128)} %param.20) | copy-start | bytes 254020
  6.2 2.3 %copy-start.8 = (f32[112,84]{0,1:T(8,128)S(1)}, f32[112,84]{0,1:T(8,128)}, u32[]{:S(2)}) copy-start(f32[112,84]{0,1:T(8,128)} %param.21) | copy-start | bytes 112900
  8.5 1.0 %copy-start.1 = (f32[9,84,128]{2,1,0:T(8,128)}, f32[9,84,128]{2,1,0:T(8,128)S(1)}, u32[]{:S(2)}) copy-start(f32[9,84,128]{2,1,0:T(8,128)S(1)} %fusion.104.refs_2_) | copy-start | bytes 1161220
  9.1 0.7 copy-start.12
  9.6 16.0 %copy-start.17 = (s32[4,128]{1,0:T(4,128)S(1)}, s32[4,128]{1,0:T(4,128)}, u32[]{:S(2)}) copy-start(s32[4,128]{1,0:T(4,128)} %param.27) | copy-start | bytes 6148
  26.5 1.1 %copy-start.10 = (s32[4,128]{1,0:T(4,128)S(1)}, s32[4,128]{1,0:T(4,128)}, u32[]{:S(2)}) copy-start(s32[4,128]{1,0:T(4,128)} %param.24) | copy-start | bytes 6148
  27.8 0.9 %copy-start.6 = (f32[4,81,128]{2,0,1:T(4,128)S(1)}, f32[4,81,128]{2,0,1:T(4,128)}, u32[]{:S(2)}) copy-start(f32[4,81,128]{2,0,1:T(4,128)} %param.19) | copy-start | bytes 497668
  27.8 1.0 %copy-start.7 = (f32[4,81,128]{2,0,1:T(4,128)S(1)}, f32[4,81,128]{2,0,1:T(4,128)}, u32[]{:S(2)}) copy-start(f32[4,81,128]{2,0,1:T(4,128)} %param.18) | copy-start | bytes 497668
  27.8 1.2 %copy-start.14 = (f32[9,84,128]{2,1,0:T(8,128)S(1)}, f32[9,84,128]{2,1,0:T(8,128)}, u32[]{:S(2)}) copy-start(f32[9,84,128]{2,1,0:T(8,128)} %get-tuple-element.8) | copy-start | bytes 1161220
  27.8 1.1 %copy-start.16 = (f32[4,84,28]{1,0,2:T(4,128)S(1)}, f32[4,84,28]{1,0,2:T(4,128)}, u32[]{:S(2)}) copy-start(f32[4,84,28]{1,0,2:T(4,128)} %param.22) | copy-start | bytes 112900
  35.4 0.9 %copy-start.2 = (f32[9,84,128]{2,1,0:T(8,128)}, f32[9,84,128]{2,1,0:T(8,128)S(1)}, u32[]{:S(2)}) copy-start(f32[9,84,128]{2,1,0:T(8,128)S(1)} %multiply_add_fusion.refs_2_) | copy-start | bytes 1161220
  50.4 1.0 %copy-start.15 = (f32[9,84,128]{2,1,0:T(8,128)S(1)}, f32[9,84,128]{2,1,0:T(8,128)}, u32[]{:S(2)}) copy-start(f32[9,84,128]{2,1,0:T(8,128)} %get-tuple-element.11) | copy-start | bytes 1161220
  50.4 1.0 %copy-start.18 = (f32[84]{0:T(128)S(1)}, f32[84]{0:T(128)}, u32[]{:S(2)}) copy-start(f32[84]{0:T(128)} %param.25) | copy-start | bytes 1012
  53.0 1.1 %copy-start.5 = (f32[2,1,9,84,128]{4,1,3,2,0:T(1,128)S(1)}, f32[2,1,9,84,128]{4,1,3,2,0:T(1,128)}, u32[]{:S(2)}) copy-start(f32[2,1,9,84,128]{4,1,3,2,0:T(1,128)} %param.16) | copy-start | bytes 2322436
  53.0 1.2 %copy-start.11 = (f32[3,81]{1,0:T(4,128)S(1)}, f32[3,81]{1,0:T(4,128)}, u32[]{:S(2)}) copy-start(f32[3,81]{1,0:T(4,128)} %param.26) | copy-start | bytes 2920
  55.3 1.2 %copy-start.13 = (s32[128]{0:T(128)S(1)}, s32[128]{0:T(128)}, u32[]{:S(2)}) copy-start(s32[128]{0:T(128)} %param.29) | copy-start | bytes 1540
  57.0 0.6 copy-start.9

commit v3 on v2

--- a/solution.py
+++ b/solution.py
@@ -127,7 +127,10 @@
     return from_prev, from_next, volume_term
 
 
-def scatter_kernel(offsets, group_count, curve_count, chunks, received, send_sem, recv_sem):
+def scatter_kernel(
+    offsets, group_count, curve_count,
+    state, weights, mixed, earlier, tile_oh, own, received, density, chunks, send_sem, recv_sem,
+):
     group = lax.axis_index("grp")
     me = lax.axis_index("curve")
     targets = [
@@ -137,6 +140,19 @@
     barrier = pltpu.get_barrier_semaphore()
     for target in targets:
         pl.semaphore_signal(barrier, inc=1, device_id=target, device_id_type=pl.DeviceIdType.MESH)
+    density[...] = jnp.zeros_like(density)
+    for param in range(3):
+        summed = earlier[pl.ds(param, 1), :]
+        for quantity in range(9):
+            weighted = state[quantity] * weights[...]
+            summed = summed + jnp.sum(weighted * mixed[param, quantity], axis=0, keepdims=True)
+        density[pl.ds(param, 1), :] = summed
+    partial = jnp.dot(density[...], tile_oh[...], precision=PRECISE, preferred_element_type=jnp.float32)
+    tile = own.shape[1]
+    own[...] = partial[:3, tile : 2 * tile]
+    for index, (shift_group, shift_curve) in enumerate(offsets):
+        start = (shift_group * 3 + shift_curve + 1) * tile
+        chunks[index] = partial[:3, start : start + tile]
     pl.semaphore_wait(barrier, len(offsets))
     copies = [
         pltpu.make_async_remote_copy(
@@ -155,7 +171,7 @@
         copy.wait()
 
 
-def scatter_tiles(partial):
+def scatter_tiles(state, weights, mixed, earlier, tile_oh):
     group_count = lax.axis_size("grp")
     curve_count = lax.axis_size("curve")
     offsets = [
@@ -164,20 +180,25 @@
         for shift_curve in (-1, 0, 1)
         if (shift_group, shift_curve) != (0, 0)
     ]
-    chunks = jnp.stack([partial[:, g, c + 1] for g, c in offsets])
+    cells = state.shape[2]
     vmem = pl.BlockSpec(memory_space=pltpu.VMEM)
-    received = pl.pallas_call(
+    own, received = pl.pallas_call(
         lambda *refs: scatter_kernel(offsets, group_count, curve_count, *refs),
-        out_shape=jax.ShapeDtypeStruct(chunks.shape, chunks.dtype),
-        in_specs=[vmem],
-        out_specs=vmem,
+        out_shape=(
+            jax.ShapeDtypeStruct((3, TILE), jnp.float32),
+            jax.ShapeDtypeStruct((len(offsets), 3, TILE), jnp.float32),
+        ),
+        in_specs=[vmem] * 5,
+        out_specs=(vmem, vmem),
         scratch_shapes=[
+            pltpu.VMEM((8, cells), jnp.float32),
+            pltpu.VMEM((len(offsets), 3, TILE), jnp.float32),
             pltpu.SemaphoreType.DMA((len(offsets),)),
             pltpu.SemaphoreType.DMA((len(offsets),)),
         ],
         compiler_params=pltpu.CompilerParams(collective_id=1, has_side_effects=True),
-    )(chunks)
-    return partial[:, 0, 1] + jnp.sum(received, axis=0)
+    )(state, weights, mixed, earlier, tile_oh)
+    return own + jnp.sum(received, axis=0)
 
 
 def on_device(
@@ -237,9 +258,10 @@
         face_flux = star(own_flux, own_trace) + star(far_flux, oriented)
         lifted = jnp.einsum("ibt,qtic->qbc", lifting, face_flux, precision=DENSE)
         state = state + volume_term - lifted
-        weighted = state * mass_weights[None, :, None]
         mixed = jnp.einsum("pqr,rbc->pqbc", mix, forward[time_step, 0], precision=DENSE)
-        density_sum = density_sum + jnp.sum(weighted[None] * mixed, axis=(1, 2))
+        if time_step < STEPS - 1:
+            weighted = state * mass_weights[None, :, None]
+            density_sum = density_sum + jnp.sum(weighted[None] * mixed, axis=(1, 2))
 
     tile = element_cell // TILE
     inside = element_cell % TILE
@@ -248,9 +270,7 @@
     slot = (rel_group * 3 + rel_curve) * TILE + inside
     slot = jnp.where(rel_curve < 3, slot, -1)
     tile_oh = (slot[:, None] == jnp.arange(group_count * 3 * TILE, dtype=jnp.int32)[None, :]).astype(f32)
-    partial = jnp.dot(density_sum, tile_oh, precision=PRECISE).reshape(3, group_count, 3, TILE)
-
-    kernel = scatter_tiles(partial)
+    kernel = scatter_tiles(state, mass_weights[:, None], mixed, density_sum, tile_oh)
     return (state.reshape(adjoint.shape), kernel[None])
 
 

time: 73.2 us -> 77.1 us (1.053)
  other arithmetic: 9.47 us -> 11.3 us
  Pallas kernels: 33.5 us -> 34.5 us
  local copies, waits for them, and re-layouts: 11.9 us -> 12.8 us
    dot_general x0 -> x1, local copies, waits for them, and re-layouts: none -> 1.44 us  [on_device(): jnp.einsum('pqr,rbc->pqbc', mix, forward[time_step, 0], precision=DENSE)]
    unnamed x57 -> x49, local copies, waits for them, and re-layouts: 7.39 us -> 6.33 us
    convert_element_type x0 -> x1, other arithmetic: none -> 1.05 us  [on_device(): (slot[:, None] == jnp.arange(group_count * 3 * TILE, dtype=jnp.int32)[Non...]
    pallas_call x1, Pallas kernels: 12.6 us -> 13.6 us  [scatter_tiles(): pl.pallas_call(lambda *refs: scatter_kernel(offsets, group_count, curve_c...]
    dot_general x2, matrix products: 2.96 us -> 3.77 us  [on_device(): lifted = jnp.einsum('ibt,qtic->qbc', lifting, face_flux, precision=DENSE)]
    dot_general x4, matrix products: 5.83 us -> 5.03 us  [predictor(): moved = jnp.einsum('dab,qbc->dqac', stiffness, derivative, precision=DENSE)]
where the time goes in v3:
time: 77.1 us; the launch traced here: 76.6 us
  Pallas kernels  34.5 us (45%)
  matrix products  16.6 us (22%)
  local copies, waits for them, and re-layouts  12.8 us (17%)
  other arithmetic  11.3 us (15%)
  between operations  1.37 us (2%)
    pallas_call x2, Pallas kernels, exchange(): pl.pallas_call(lambda *refs: exchange_kernel(count, *refs), out_shape=(ja...  20.9 us
    pallas_call x1, Pallas kernels, scatter_tiles(): pl.pallas_call(lambda *refs: scatter_kernel(offsets, group_count, curve_c...  13.6 us
    unnamed x49, local copies, waits for them, and re-layouts  6.33 us
    dot_general x4, matrix products, predictor(): moved = jnp.einsum('dab,qbc->dqac', stiffness, derivative, precision=DENSE)  5.03 us
    add x2, other arithmetic, predictor(): integral = integral + factor * derivative  4.73 us
    dot_general x2, matrix products, on_device(): lifted = jnp.einsum('ibt,qtic->qbc', lifting, face_flux, precision=DENSE)  3.77 us
    dot_general x2, matrix products, on_device(): jnp.einsum('pqr,rbc->pqbc', mix, forward[time_step, 0], precision=DENSE)  2.56 us
    dot_general x2, matrix products, on_device(): jnp.dot(extended, gather_oh, precision=PRECISE)  1.86 us

profile of v3, /device:TPU:1, one launch (start us, length us, event | category | flops | bytes accessed | tf_op | source)
XLA Modules:
  0.0 76.6 jit_solution(12876853614035167936)
XLA Ops:
  0.6 0.0 copy-start
  0.7 0.9 %fusion.210 = (f32[1,81,128]{2,1,0:T(8,128)S(1)}, f32[1,81,128]{2,1,0:T(8,128)S(1)}, f32[1,81,128]{2,1,0:T(8,128)S(1)}) fusion(f32[3,81,128]{2,1,0:T(8,128)} %refs_4_.3), kind=kLoop, calls=%fused_computation.455 | loop fusion | bytes 248832 | tf_op jit(solution)/shard_map/slice | solution.py:28
  1.9 0.7 convolution_bitcast_fusion.5
  2.6 0.1 slice_bitcast_fusion.149
  2.7 1.8 %convolution_bitcast_fusion.4 = f32[3,9,84,128]{3,2,0,1:T(8,128)S(1)} fusion(f32[3,84,84]{2,1,0:T(8,128)S(1)} %copy-done.5, f32[84,128]{1,0:T(8,128)S(1)} %get-tuple-element.104, f32[9,128]{1,0:T(8,128)S(1)} %get-tuple-element.227, f32[84,128]{1,0:T(8,128)S(1)} %get-tuple-element.105, f32[9,128]{1,0:T(8,128)S(1)} %get-tuple-element.228, ...), kind=kOutput, calls=%fused_computation.8 | convolution fusion | flops 151441920 | bytes 2531520 | tf_op jit(solution)/shard_map/dab,qbc->dqac/dot_general | solution.py:39
  4.5 0.1 slice_bitcast_fusion.122
  4.7 2.4 %fusion.105.refs_2_ = f32[9,84,128]{2,1,0:T(8,128)S(1)} fusion(f32[1,9,84,128]{3,0,2,1:T(1,128)S(1)} %copy-done.3, f32[84,128]{1,0:T(8,128)S(1)} %get-tuple-element.77, f32[84,128]{1,0:T(8,128)S(1)} %get-tuple-element.78, f32[84,128]{1,0:T(8,128)S(1)} %get-tuple-element.79, f32[84,128]{1,0:T(8,128)S(1)} %get-tuple-element.80, ...), kind=kLoop, calls=%fused_computation.129 | loop fusion | flops 10741248 | bytes 3220992 | tf_op jit(solution)/shard_map/add | solution.py:42
  7.1 0.1 copy.88
  7.2 0.4 convolution_bitcast_fusion.7
  7.6 0.3 copy.89
  7.9 0.0 copy-start.12
  7.9 0.1 pad.8
  8.1 0.5 copy-done.12
  8.6 0.4 fusion.102
  9.1 0.0 copy-start.18
  9.1 0.7 fusion.209
  9.8 0.8 %copy.90 = f32[3,84,84]{1,2,0:T(8,128)} copy(f32[3,84,84]{2,1,0:T(8,128)S(1)} %copy-done.5) | data formatting | bytes 169344 | tf_op args[5]
  10.6 12.0 %shard_map.158 = (f32[252,128]{1,0:T(8,128)}, f32[252,128]{1,0:T(8,128)}, f32[9,84,128]{2,1,0:T(8,128)}) custom-call(f32[252,128]{1,0:T(8,128)} %get-tuple-element.171.refs_0_, f32[252,128]{1,0:T(8,128)} %get-tuple-element.170.refs_1_, f32[9,84,128]{2,1,0:T(8,128)} %copy-done.1, f32[3,84,84]{2,1,0:T(8,128)} %bitcast.575, f32[3,81,128]{2,1,0:T(8,128)} %refs_4_.3), custom_call_target="tpu_custom_call" | custom-call | tf_op jit(solution)/shard_map/pallas_call | solution.py:113
  22.5 0.9 %broadcast_select_fusion.2 = f32[252,128]{1,0:T(8,128)S(1)} fusion(f32[252,128]{1,0:T(8,128)} %get-tuple-element.12, pred[]{:T(512)S(6)} %eq.74), kind=kLoop, calls=%fused_computation.260 | loop fusion | flops 32256 | bytes 258049 | tf_op jit(solution)/shard_map/jit(_where)/select_n | solution.py:126
  23.5 0.9 %broadcast_select_fusion.3 = f32[252,128]{1,0:T(8,128)S(1)} fusion(f32[252,128]{1,0:T(8,128)} %get-tuple-element.11, pred[]{:T(512)S(6)} %eq.73), kind=kLoop, calls=%fused_computation.261 | loop fusion | flops 32256 | bytes 258049 | tf_op jit(solution)/shard_map/jit(_where)/select_n | solution.py:125
  24.4 0.9 %fusion.1 = f32[252,512]{1,0:T(8,128)S(1)} fusion(f32[252,128]{1,0:T(8,128)S(1)} %broadcast_select_fusion.2, f32[252,128]{1,0:T(8,128)S(1)} %broadcast_select_fusion.3, f32[252,512]{1,0:T(8,128)S(1)} %bitcast.567, s32[512]{0:T(512)S(1)} %bitcast.584), kind=kOutput, calls=%fused_computation.3 | convolution fusion | flops 1189865472 | bytes 1292288 | tf_op jit(solution)/shard_map/dot_general | solution.py:256
  25.3 0.2 reshape.268
  25.5 0.8 %convolution_bitcast_fusion.1 = f32[3,9,28,4,128]{4,2,0,3,1:T(8,128)S(1)} fusion(f32[9,28,4,128,1]{3,2,1,0,4:T(4,128)S(1)} %bitcast.565, f32[3,28,28]{2,1,0:T(8,128)S(1)} %copy-done), kind=kOutput, calls=%fused_computation.5 | convolution fusion | flops 65028096 | bytes 2073792 | tf_op jit(solution)/shard_map/rts,qsic->rqtic/dot_general | solution.py:52
  26.4 0.2 fusion.24
  26.7 0.0 copy-start.13
  26.7 0.0 copy-start.17
  26.8 0.8 copy-done.7
  27.5 0.1 copy-done.8
  27.6 0.1 slice_bitcast_fusion.158
  27.7 0.1 copy-done.15
  27.8 1.5 %broadcast_multiply_fusion = (f32[9,84,128]{2,1,0:T(8,128)S(1)}, f32[9,84,128]{2,1,0:T(8,128)S(1)}) fusion(f32[84]{0:T(128)S(1)} %copy-done.13, f32[4,84,28]{1,0,2:T(4,128)S(1)} %copy-done.17, f32[28,4,128]{2,0,1:T(8,128)S(1)} %get-tuple-element.160, f32[9,4,128]{2,1,0:T(4,128)S(1)} %get-tuple-element.182, f32[28,4,128]{2,0,1:T(8,128)S(1)} %get-tuple-element.161, ...), kind=kOutput, calls=%fused_computation.213 | convolution fusion | flops 69834240 | bytes 2950224 | tf_op jit(solution)/shard_map/ibt,qtic->qbc/dot_general | solution.py:259
  29.3 0.7 convolution_bitcast_fusion.3
  30.0 0.1 slice_bitcast_fusion.95
  30.1 1.8 %convolution_bitcast_fusion.2 = f32[3,9,84,128]{3,2,0,1:T(8,128)S(1)} fusion(f32[3,84,84]{2,1,0:T(8,128)S(1)} %copy-done.5, f32[84,128]{1,0:T(8,128)S(1)} %get-tuple-element.50, f32[84,128]{1,0:T(8,128)S(1)} %get-tuple-element.51, f32[84,128]{1,0:T(8,128)S(1)} %get-tuple-element.52, f32[84,128]{1,0:T(8,128)S(1)} %get-tuple-element.53, ...), kind=kOutput, calls=%fused_computation.6 | convolution fusion | flops 151441920 | bytes 2531520 | tf_op jit(solution)/shard_map/dab,qbc->dqac/dot_general | solution.py:39
  32.0 0.1 slice_bitcast_fusion.68
  32.1 2.4 %multiply_add_fusion.refs_2_ = f32[9,84,128]{2,1,0:T(8,128)S(1)} fusion(f32[9,84,128]{2,1,0:T(8,128)S(1)} %get-tuple-element.226, f32[84,128]{1,0:T(8,128)S(1)} %get-tuple-element.23, f32[84,128]{1,0:T(8,128)S(1)} %get-tuple-element.24, f32[84,128]{1,0:T(8,128)S(1)} %get-tuple-element.25, f32[84,128]{1,0:T(8,128)S(1)} %get-tuple-element.26, ...), kind=kLoop, calls=%fused_computation.135 | loop fusion | flops 10741248 | bytes 3220992 | tf_op jit(solution)/shard_map/add | solution.py:42
  34.5 0.4 convolution_bitcast_fusion.6
  34.9 0.3 copy.95
  35.2 0.1 pad.9
  35.4 0.4 fusion.101
  35.8 0.7 fusion.208
  36.5 8.9 %shard_map.159 = (f32[252,128]{1,0:T(8,128)}, f32[252,128]{1,0:T(8,128)}, f32[9,84,128]{2,1,0:T(8,128)}) custom-call(f32[252,128]{1,0:T(8,128)} %get-tuple-element.169.refs_0_, f32[252,128]{1,0:T(8,128)} %get-tuple-element.168.refs_1_, f32[9,84,128]{2,1,0:T(8,128)} %copy-done.2, f32[3,84,84]{2,1,0:T(8,128)} %bitcast.576, f32[3,81,128]{2,1,0:T(8,128)} %refs_4_.3), custom_call_target="tpu_custom_call" | custom-call | tf_op jit(solution)/shard_map/pallas_call | solution.py:113
  45.5 0.9 %broadcast_select_fusion.1 = f32[252,128]{1,0:T(8,128)S(1)} fusion(f32[252,128]{1,0:T(8,128)} %get-tuple-element.14, pred[]{:T(512)S(6)} %eq.73), kind=kLoop, calls=%fused_computation.259 | loop fusion | flops 32256 | bytes 258049 | tf_op jit(solution)/shard_map/jit(_where)/select_n | solution.py:125
  46.4 0.9 %broadcast_select_fusion = f32[252,128]{1,0:T(8,128)S(1)} fusion(f32[252,128]{1,0:T(8,128)} %get-tuple-element.15, pred[]{:T(512)S(6)} %eq.74), kind=kLoop, calls=%fused_computation.258 | loop fusion | flops 32256 | bytes 258049 | tf_op jit(solution)/shard_map/jit(_where)/select_n | solution.py:126
  47.3 0.9 %fusion = f32[252,512]{1,0:T(8,128)S(1)} fusion(f32[252,128]{1,0:T(8,128)S(1)} %broadcast_select_fusion, f32[252,128]{1,0:T(8,128)S(1)} %broadcast_select_fusion.1, f32[252,512]{1,0:T(8,128)S(1)} %bitcast.569, s32[512]{0:T(512)S(1)} %bitcast.585), kind=kOutput, calls=%fused_computation.2 | convolution fusion | flops 1189865472 | bytes 1292288 | tf_op jit(solution)/shard_map/dot_general | solution.py:256
  48.3 0.2 reshape.270
  48.4 0.8 %convolution_bitcast_fusion = f32[3,9,28,4,128]{4,2,3,1,0:T(8,128)S(1)} fusion(f32[9,28,4,128]{3,2,1,0:T(4,128)S(1)} %reshape.270, f32[3,28,28]{2,1,0:T(8,128)S(1)} %copy-done), kind=kOutput, calls=%fused_computation.4 | convolution fusion | flops 65028096 | bytes 2073792 | tf_op jit(solution)/shard_map/rts,qsic->rqtic/dot_general | solution.py:52
  49.3 0.2 fusion.19
  49.6 0.9 %copy-done.16 = f32[9,84,128]{2,1,0:T(8,128)S(1)} copy-done((f32[9,84,128]{2,1,0:T(8,128)S(1)}, f32[9,84,128]{2,1,0:T(8,128)}, u32[]{:S(2)}) %copy-start.16) | copy-done | bytes 387096
  50.5 2.3 %fusion.3.refs_0_ = f32[9,84,128]{2,1,0:T(8,128)} fusion(f32[9,84,128]{2,1,0:T(8,128)S(1)} %get-tuple-element.226, f32[9,84,128]{2,1,0:T(8,128)S(1)} %copy-done.16, f32[28,4,128]{2,0,1:T(8,128)S(1)} %get-tuple-element.142, f32[28,4,128]{2,0,1:T(8,128)S(1)} %get-tuple-element.143, f32[28,4,128]{2,0,1:T(8,128)S(1)} %get-tuple-element.144, ...), kind=kOutput, calls=%fused_computation.15 | convolution fusion | flops 69737472 | bytes 2562816 | tf_op jit(solution)/shard_map/ibt,qtic->qbc/dot_general | solution.py:259
  52.8 0.1 copy.100
  52.9 1.0 %copy-done.6 = f32[2,1,9,84,128]{4,1,3,2,0:T(1,128)S(1)} copy-done((f32[2,1,9,84,128]{4,1,3,2,0:T(1,128)S(1)}, f32[2,1,9,84,128]{4,1,3,2,0:T(1,128)}, u32[]{:S(2)}) %copy-start.6) | copy-done | bytes 774168
  53.9 0.1 fusion.207
  54.0 0.1 reshape.288
  54.1 1.6 %multiply_reduce_fusion.refs_3_ = f32[3,128]{1,0:T(4,128)} fusion(f32[9,84,128]{2,0,1:T(8,128)S(1)} %copy.100, f32[1,1,9,84,128]{4,1,3,2,0:T(1,128)S(1)} %get-tuple-element.130, f32[3,9,9,1]{2,1,0,3:T(8,128)S(1)} %reshape.288), kind=kOutput, calls=%fused_computation | convolution fusion | flops 16256640 | bytes 776652 | tf_op jit(solution)/shard_map/pqr,rbc->pqbc/dot_general | solution.py:261
  55.7 1.0 %fusion.16.refs_4_ = f32[128,1536]{1,0:T(8,128)} fusion(s32[128]{0:T(128)S(1)} %compare_select_fusion.4), kind=kLoop, calls=%fused_computation.29 | loop fusion | flops 393216 | bytes 786944 | tf_op jit(solution)/shard_map/convert_element_type | solution.py:272
  56.8 0.9 %fusion.17 = f32[3,9,84,128]{3,1,2,0:T(8,128)S(1)} fusion(f32[1,1,9,84,128]{4,1,3,2,0:T(1,128)S(1)} %get-tuple-element.131, f32[3,9,9,1]{2,1,0,3:T(8,128)S(1)} %reshape.288), kind=kOutput, calls=%fused_computation.32 | convolution fusion | flops 15676416 | bytes 1549260 | tf_op jit(solution)/shard_map/pqr,rbc->pqbc/dot_general | solution.py:261
  57.7 1.4 %copy.103.refs_2_ = f32[3,9,84,128]{3,2,1,0:T(8,128)} copy(f32[3,9,84,128]{3,1,2,0:T(8,128)S(1)} %fusion.17) | data formatting | bytes 2322432 | tf_op jit(solution)/shard_map/pqr,rbc->pqbc/dot_general | solution.py:261
  59.1 0.7 copy.102.refs_1_
  59.9 13.6 %shard_map.160 = (f32[3,128]{1,0:T(4,128)}, f32[11,3,128]{2,1,0:T(4,128)}) custom-call(f32[9,84,128]{2,1,0:T(8,128)} %fusion.3.refs_0_, f32[84,1]{1,0:T(8,128)} %copy.102.refs_1_, f32[3,9,84,128]{3,2,1,0:T(8,128)} %copy.103.refs_2_, f32[3,128]{1,0:T(4,128)} %multiply_reduce_fusion.refs_3_, f32[128,1536]{1,0:T(8,128)} %fusion.16.refs_4_), custom_call_target="tpu_custom_call" | custom-call | tf_op jit(solution)/shard_map/pallas_call | solution.py:185
  73.5 0.8 reduce_sum.19
  74.2 0.7 add_bitcast_fusion
  74.9 0.6 copy.105
  75.5 1.1 %copy.104 = f32[1,9,84,128]{3,0,2,1:T(1,128)} copy(f32[1,9,84,128]{3,2,1,0:T(8,128)S(1)} %bitcast.574) | data formatting | bytes 774144
  (64 shorter events, 0.6 us)
Async XLA Ops:
  0.6 24.9 %copy-start = (f32[3,28,28]{2,1,0:T(8,128)S(1)}, f32[3,28,28]{2,1,0:T(8,128)}, u32[]{:S(2)}) copy-start(f32[3,28,28]{2,1,0:T(8,128)} %param.23) | copy-start | bytes 28228
  0.6 1.2 %copy-start.3 = (f32[1,9,84,128]{3,0,2,1:T(1,128)S(1)}, f32[1,9,84,128]{3,0,2,1:T(1,128)}, u32[]{:S(2)}) copy-start(f32[1,9,84,128]{3,0,2,1:T(1,128)} %param.15) | copy-start | bytes 1161220
  0.7 1.2 %copy-start.5 = (f32[3,84,84]{2,1,0:T(8,128)S(1)}, f32[3,84,84]{2,1,0:T(8,128)}, u32[]{:S(2)}) copy-start(f32[3,84,84]{2,1,0:T(8,128)} %param.20) | copy-start | bytes 254020
  4.7 2.4 %copy-start.9 = (f32[112,84]{0,1:T(8,128)S(1)}, f32[112,84]{0,1:T(8,128)}, u32[]{:S(2)}) copy-start(f32[112,84]{0,1:T(8,128)} %param.21) | copy-start | bytes 112900
  7.0 1.0 %copy-start.1 = (f32[9,84,128]{2,1,0:T(8,128)}, f32[9,84,128]{2,1,0:T(8,128)S(1)}, u32[]{:S(2)}) copy-start(f32[9,84,128]{2,1,0:T(8,128)S(1)} %fusion.105.refs_2_) | copy-start | bytes 1161220
  7.9 0.7 copy-start.12
  9.1 15.3 %copy-start.18 = (s32[4,128]{1,0:T(4,128)S(1)}, s32[4,128]{1,0:T(4,128)}, u32[]{:S(2)}) copy-start(s32[4,128]{1,0:T(4,128)} %param.27) | copy-start | bytes 6148
  25.5 0.9 %copy-start.10 = (s32[4,128]{1,0:T(4,128)S(1)}, s32[4,128]{1,0:T(4,128)}, u32[]{:S(2)}) copy-start(s32[4,128]{1,0:T(4,128)} %param.24) | copy-start | bytes 6148
  26.6 0.9 %copy-start.7 = (f32[4,81,128]{2,0,1:T(4,128)S(1)}, f32[4,81,128]{2,0,1:T(4,128)}, u32[]{:S(2)}) copy-start(f32[4,81,128]{2,0,1:T(4,128)} %param.19) | copy-start | bytes 497668
  26.6 1.0 %copy-start.8 = (f32[4,81,128]{2,0,1:T(4,128)S(1)}, f32[4,81,128]{2,0,1:T(4,128)}, u32[]{:S(2)}) copy-start(f32[4,81,128]{2,0,1:T(4,128)} %param.18) | copy-start | bytes 497668
  26.7 1.0 %copy-start.13 = (f32[84]{0:T(128)S(1)}, f32[84]{0:T(128)}, u32[]{:S(2)}) copy-start(f32[84]{0:T(128)} %param.25) | copy-start | bytes 1012
  26.7 1.1 %copy-start.15 = (f32[9,84,128]{2,1,0:T(8,128)S(1)}, f32[9,84,128]{2,1,0:T(8,128)}, u32[]{:S(2)}) copy-start(f32[9,84,128]{2,1,0:T(8,128)} %get-tuple-element.10) | copy-start | bytes 1161220
  26.7 1.1 %copy-start.17 = (f32[4,84,28]{1,0,2:T(4,128)S(1)}, f32[4,84,28]{1,0,2:T(4,128)}, u32[]{:S(2)}) copy-start(f32[4,84,28]{1,0,2:T(4,128)} %param.22) | copy-start | bytes 112900
  34.4 0.9 %copy-start.2 = (f32[9,84,128]{2,1,0:T(8,128)}, f32[9,84,128]{2,1,0:T(8,128)S(1)}, u32[]{:S(2)}) copy-start(f32[9,84,128]{2,1,0:T(8,128)S(1)} %multiply_add_fusion.refs_2_) | copy-start | bytes 1161220
  35.4 12.0 %copy-start.19 = (s32[4,128]{1,0:T(4,128)S(1)}, s32[4,128]{1,0:T(4,128)}, u32[]{:S(2)}) copy-start(s32[4,128]{1,0:T(4,128)} %param.27) | copy-start | bytes 6148
  49.5 1.0 %copy-start.16 = (f32[9,84,128]{2,1,0:T(8,128)S(1)}, f32[9,84,128]{2,1,0:T(8,128)}, u32[]{:S(2)}) copy-start(f32[9,84,128]{2,1,0:T(8,128)} %get-tuple-element.13) | copy-start | bytes 1161220
  52.8 1.1 %copy-start.6 = (f32[2,1,9,84,128]{4,1,3,2,0:T(1,128)S(1)}, f32[2,1,9,84,128]{4,1,3,2,0:T(1,128)}, u32[]{:S(2)}) copy-start(f32[2,1,9,84,128]{4,1,3,2,0:T(1,128)} %param.16) | copy-start | bytes 2322436
  52.8 1.2 %copy-start.11 = (f32[3,81]{1,0:T(4,128)S(1)}, f32[3,81]{1,0:T(4,128)}, u32[]{:S(2)}) copy-start(f32[3,81]{1,0:T(4,128)} %param.26) | copy-start | bytes 2920
  53.9 1.8 %copy-start.14 = (s32[128]{0:T(128)S(1)}, s32[128]{0:T(128)}, u32[]{:S(2)}) copy-start(s32[128]{0:T(128)} %param.29) | copy-start | bytes 1540
  59.9 15.6 %copy-start.4 = (f32[9,84,128]{2,1,0:T(8,128)S(1)}, f32[9,84,128]{2,1,0:T(8,128)}, u32[]{:S(2)}) copy-start(f32[9,84,128]{2,1,0:T(8,128)} %fusion.3.refs_0_) | copy-start | bytes 1161220

commit v4 on v2

--- a/solution.py
+++ b/solution.py
@@ -75,42 +75,72 @@
 ):
     group = lax.axis_index("grp")
     me = lax.axis_index("curve")
-    right, left = lax.rem(me + 1, count), lax.rem(me + count - 1, count)
+    has_left = me > 0
+    has_right = me < count - 1
     barrier = pltpu.get_barrier_semaphore()
-    for side in (left, right):
-        pl.semaphore_signal(barrier, inc=1, device_id=(group, side), device_id_type=pl.DeviceIdType.MESH)
+
+    @pl.when(has_left)
+    def _():
+        pl.semaphore_signal(barrier, inc=1, device_id=(group, me - 1), device_id_type=pl.DeviceIdType.MESH)
+
+    @pl.when(has_right)
+    def _():
+        pl.semaphore_signal(barrier, inc=1, device_id=(group, me + 1), device_id_type=pl.DeviceIdType.MESH)
+
+    @pl.when(me == 0)
+    def _():
+        from_prev[...] = jnp.zeros_like(from_prev)
+
+    @pl.when(me == count - 1)
+    def _():
+        from_next[...] = jnp.zeros_like(from_next)
+
     add_volume(integral, stiff_t, mats, volume_out, (0,))
-    pl.semaphore_wait(barrier, 2)
-    copies = [
-        pltpu.make_async_remote_copy(
-            src_ref=to_next,
-            dst_ref=from_prev,
-            send_sem=send_sem.at[0],
-            recv_sem=recv_sem.at[0],
-            device_id=(group, right),
-            device_id_type=pl.DeviceIdType.MESH,
-        ),
-        pltpu.make_async_remote_copy(
-            src_ref=to_prev,
-            dst_ref=from_next,
-            send_sem=send_sem.at[1],
-            recv_sem=recv_sem.at[1],
-            device_id=(group, left),
-            device_id_type=pl.DeviceIdType.MESH,
-        ),
-    ]
-    for copy in copies:
-        copy.start()
+    to_right = pltpu.make_async_remote_copy(
+        src_ref=to_next,
+        dst_ref=from_prev,
+        send_sem=send_sem.at[0],
+        recv_sem=recv_sem.at[0],
+        device_id=(group, lax.rem(me + 1, count)),
+        device_id_type=pl.DeviceIdType.MESH,
+    )
+    to_left = pltpu.make_async_remote_copy(
+        src_ref=to_prev,
+        dst_ref=from_next,
+        send_sem=send_sem.at[1],
+        recv_sem=recv_sem.at[1],
+        device_id=(group, lax.rem(me + count - 1, count)),
+        device_id_type=pl.DeviceIdType.MESH,
+    )
+
+    neighbours = (me + count - 1) // count + (2 * count - 2 - me) // count
+    pl.semaphore_wait(barrier, neighbours)
+
+    @pl.when(has_right)
+    def _():
+        to_right.start()
+
+    @pl.when(has_left)
+    def _():
+        to_left.start()
+
     add_volume(integral, stiff_t, mats, volume_out, (1, 2))
-    for copy in copies:
-        copy.wait()
+
+    @pl.when(has_right)
+    def _():
+        to_right.wait_send()
+        to_left.wait_recv()
+
+    @pl.when(has_left)
+    def _():
+        to_left.wait_send()
+        to_right.wait_recv()
 
 
 def exchange(to_next, to_prev, integral, stiff_t, star_mats):
     count = lax.axis_size("curve")
-    me = lax.axis_index("curve")
     vmem = pl.BlockSpec(memory_space=pltpu.VMEM)
-    from_prev, from_next, volume_term = pl.pallas_call(
+    return pl.pallas_call(
         lambda *refs: exchange_kernel(count, *refs),
         out_shape=(
             jax.ShapeDtypeStruct(to_next.shape, to_next.dtype),
@@ -122,9 +152,6 @@
         scratch_shapes=[pltpu.SemaphoreType.DMA((2,)), pltpu.SemaphoreType.DMA((2,))],
         compiler_params=pltpu.CompilerParams(collective_id=0, has_side_effects=True),
     )(to_next, to_prev, integral, stiff_t, star_mats)
-    from_prev = jnp.where(me == 0, 0.0, from_prev)
-    from_next = jnp.where(me == count - 1, 0.0, from_next)
-    return from_prev, from_next, volume_term
 
 
 def scatter_kernel(offsets, group_count, curve_count, chunks, received, send_sem, recv_sem):

time: 73.2 us -> 68.4 us (0.934)
  the two profiles are of different devices: /device:TPU:1 before, /device:TPU:103 now
where the time goes in v4:
time: 68.4 us; the launch traced here: 67.9 us
  Pallas kernels  30.9 us (45%)
  matrix products  18 us (26%)
  local copies, waits for them, and re-layouts  11.9 us (17%)
  other arithmetic  5.78 us (8%)
  between operations  1.39 us (2%)
    pallas_call x2, Pallas kernels, exchange(): pl.pallas_call(lambda *refs: exchange_kernel(count, *refs), out_shape=(ja...  19.6 us
    pallas_call x1, Pallas kernels, scatter_tiles(): pl.pallas_call(lambda *refs: scatter_kernel(offsets, group_count, curve_c...  11.3 us
    unnamed x57, local copies, waits for them, and re-layouts  7.39 us
    dot_general x4, matrix products, predictor(): moved = jnp.einsum('dab,qbc->dqac', stiffness, derivative, precision=DENSE)  5.82 us
    add x2, other arithmetic, predictor(): integral = integral + factor * derivative  4.56 us
    dot_general x2, matrix products, on_device(): jnp.dot(extended, gather_oh, precision=PRECISE)  3.79 us
    dot_general x2, matrix products, on_device(): lifted = jnp.einsum('ibt,qtic->qbc', lifting, face_flux, precision=DENSE)  2.57 us
    dot_general x2, matrix products, on_device(): jnp.einsum('pqr,rbc->pqbc', mix, forward[time_step, 0], precision=DENSE)  2.04 us

profile of v4, /device:TPU:103, one launch (start us, length us, event | category | flops | bytes accessed | tf_op | source)
XLA Modules:
  0.0 67.9 jit_solution(1701511173355069960)
XLA Ops:
  0.6 0.0 copy-start
  0.7 0.9 %fusion.212 = (f32[1,81,128]{2,1,0:T(8,128)S(1)}, f32[1,81,128]{2,1,0:T(8,128)S(1)}, f32[1,81,128]{2,1,0:T(8,128)S(1)}) fusion(f32[3,81,128]{2,1,0:T(8,128)} %refs_4_.3), kind=kLoop, calls=%fused_computation.477 | loop fusion | bytes 248832 | tf_op jit(solution)/shard_map/slice | solution.py:28
  1.9 1.6 %convolution_bitcast_fusion.5 = f32[3,9,84,128]{3,2,0,1:T(8,128)S(1)} fusion(f32[1,9,84,128]{3,0,2,1:T(1,128)S(1)} %copy-done.3, f32[3,84,84]{2,1,0:T(8,128)} %param.20), kind=kOutput, calls=%fused_computation.10 | convolution fusion | flops 146313216 | bytes 1632960 | tf_op jit(solution)/shard_map/dab,qbc->dqac/dot_general | solution.py:39
  3.5 0.0 copy-start.4
  3.5 0.1 slice_bitcast_fusion.149
  3.6 0.8 %copy-done.4 = f32[3,84,84]{2,1,0:T(8,128)S(1)} copy-done((f32[3,84,84]{2,1,0:T(8,128)S(1)}, f32[3,84,84]{2,1,0:T(8,128)}, u32[]{:S(2)}) %copy-start.4) | copy-done | bytes 84696
  4.4 1.8 %convolution_bitcast_fusion.4 = f32[3,9,84,128]{3,2,0,1:T(8,128)S(1)} fusion(f32[3,84,84]{2,1,0:T(8,128)S(1)} %copy-done.4, f32[84,128]{1,0:T(8,128)S(1)} %get-tuple-element.102, f32[9,128]{1,0:T(8,128)S(1)} %get-tuple-element.226, f32[84,128]{1,0:T(8,128)S(1)} %get-tuple-element.103, f32[9,128]{1,0:T(8,128)S(1)} %get-tuple-element.227, ...), kind=kOutput, calls=%fused_computation.9 | convolution fusion | flops 151441920 | bytes 2531520 | tf_op jit(solution)/shard_map/dab,qbc->dqac/dot_general | solution.py:39
  6.1 0.1 slice_bitcast_fusion.122
  6.2 0.0 copy-start.8
  6.3 2.3 %fusion.104.refs_2_ = f32[9,84,128]{2,1,0:T(8,128)S(1)} fusion(f32[1,9,84,128]{3,0,2,1:T(1,128)S(1)} %copy-done.3, f32[84,128]{1,0:T(8,128)S(1)} %get-tuple-element.75, f32[84,128]{1,0:T(8,128)S(1)} %get-tuple-element.76, f32[84,128]{1,0:T(8,128)S(1)} %get-tuple-element.77, f32[84,128]{1,0:T(8,128)S(1)} %get-tuple-element.78, ...), kind=kLoop, calls=%fused_computation.129 | loop fusion | flops 10741248 | bytes 3220992 | tf_op jit(solution)/shard_map/add | solution.py:42
  8.6 0.1 copy.123
  8.7 0.4 convolution_bitcast_fusion.7
  9.1 0.0 copy-start.12
  9.1 0.3 copy.124
  9.4 0.1 pad.8
  9.5 0.0 copy-start.17
  9.6 0.2 copy-done.12
  9.8 0.4 fusion.101
  10.2 0.7 %fusion.211 = (f32[252,128]{1,0:T(8,128)}, f32[252,128]{1,0:T(8,128)}) fusion(f32[252,256]{1,0:T(8,128)S(1)} %fusion.101), kind=kLoop, calls=%fused_computation.476 | loop fusion | bytes 516096 | tf_op jit(solution)/shard_map/slice | solution.py:259
  10.9 0.8 %copy.125 = f32[3,84,84]{1,2,0:T(8,128)} copy(f32[3,84,84]{2,1,0:T(8,128)S(1)} %copy-done.4) | data formatting | bytes 169344 | tf_op args[5]
  11.7 9.8 %shard_map.158 = (f32[252,128]{1,0:T(8,128)}, f32[252,128]{1,0:T(8,128)}, f32[9,84,128]{2,1,0:T(8,128)}) custom-call(f32[252,128]{1,0:T(8,128)} %get-tuple-element.169.refs_0_, f32[252,128]{1,0:T(8,128)} %get-tuple-element.168.refs_1_, f32[9,84,128]{2,1,0:T(8,128)} %copy-done.1, f32[3,84,84]{2,1,0:T(8,128)} %bitcast.622, f32[3,81,128]{2,1,0:T(8,128)} %refs_4_.3), custom_call_target="tpu_custom_call" | custom-call | tf_op jit(solution)/shard_map/pallas_call | solution.py:143
  21.6 1.9 %fusion.1 = f32[252,512]{1,0:T(8,128)S(1)} fusion(f32[252,128]{1,0:T(8,128)} %get-tuple-element.10, f32[252,128]{1,0:T(8,128)} %get-tuple-element.9, f32[252,512]{1,0:T(8,128)S(1)} %bitcast.615, s32[512]{0:T(512)S(1)} %bitcast.643), kind=kOutput, calls=%fused_computation.4 | convolution fusion | flops 1189865472 | bytes 1292288 | tf_op jit(solution)/shard_map/dot_general | solution.py:262
  23.5 0.0 copy-start.10
  23.5 0.2 reshape.286
  23.7 0.8 %convolution_bitcast_fusion.1 = f32[3,9,28,4,128]{4,2,0,3,1:T(8,128)S(1)} fusion(f32[9,28,4,128,1]{3,2,1,0,4:T(4,128)S(1)} %bitcast.613, f32[3,28,28]{2,1,0:T(8,128)S(1)} %copy-done), kind=kOutput, calls=%fused_computation.6 | convolution fusion | flops 65028096 | bytes 2073792 | tf_op jit(solution)/shard_map/rts,qsic->rqtic/dot_general | solution.py:52
  24.5 0.2 fusion.23
  24.8 0.0 copy-start.16
  24.9 0.8 %copy-done.6 = f32[4,81,128]{2,0,1:T(4,128)S(1)} copy-done((f32[4,81,128]{2,0,1:T(4,128)S(1)}, f32[4,81,128]{2,0,1:T(4,128)}, u32[]{:S(2)}) %copy-start.6) | copy-done | bytes 165912
  25.7 0.1 copy-done.7
  25.8 0.1 slice_bitcast_fusion.158
  25.8 0.1 copy-done.15
  25.9 1.3 %fusion.2 = f32[9,84,128]{2,1,0:T(8,128)S(1)} fusion(f32[9,84,128]{2,1,0:T(8,128)S(1)} %copy-done.15, f32[1,9,84,128]{3,0,2,1:T(1,128)S(1)} %copy-done.3, f32[28,4,128]{2,0,1:T(8,128)S(1)} %get-tuple-element.158, f32[9,4,128]{2,1,0:T(4,128)S(1)} %get-tuple-element.180, f32[28,4,128]{2,0,1:T(8,128)S(1)} %get-tuple-element.159, ...), kind=kOutput, calls=%fused_computation.15 | convolution fusion | flops 69737472 | bytes 2562816 | tf_op jit(solution)/shard_map/ibt,qtic->qbc/dot_general | solution.py:265
  27.2 0.7 convolution_bitcast_fusion.3
  27.9 0.1 slice_bitcast_fusion.95
  28.0 1.8 %convolution_bitcast_fusion.2 = f32[3,9,84,128]{3,2,0,1:T(8,128)S(1)} fusion(f32[3,84,84]{2,1,0:T(8,128)S(1)} %copy-done.4, f32[84,128]{1,0:T(8,128)S(1)} %get-tuple-element.48, f32[84,128]{1,0:T(8,128)S(1)} %get-tuple-element.49, f32[84,128]{1,0:T(8,128)S(1)} %get-tuple-element.50, f32[84,128]{1,0:T(8,128)S(1)} %get-tuple-element.51, ...), kind=kOutput, calls=%fused_computation.7 | convolution fusion | flops 151441920 | bytes 2531520 | tf_op jit(solution)/shard_map/dab,qbc->dqac/dot_general | solution.py:39
  29.8 0.1 slice_bitcast_fusion.68
  29.9 2.3 %multiply_add_fusion.refs_2_ = f32[9,84,128]{2,1,0:T(8,128)S(1)} fusion(f32[9,84,128]{2,1,0:T(8,128)S(1)} %fusion.2, f32[84,128]{1,0:T(8,128)S(1)} %get-tuple-element.21, f32[84,128]{1,0:T(8,128)S(1)} %get-tuple-element.22, f32[84,128]{1,0:T(8,128)S(1)} %get-tuple-element.23, f32[84,128]{1,0:T(8,128)S(1)} %get-tuple-element.24, ...), kind=kLoop, calls=%fused_computation.135 | loop fusion | flops 10741248 | bytes 3220992 | tf_op jit(solution)/shard_map/add | solution.py:42
  32.2 0.4 convolution_bitcast_fusion.6
  32.6 0.3 copy.130
  32.9 0.1 pad.9
  33.1 0.4 fusion.100
  33.5 0.7 %fusion.210 = (f32[252,128]{1,0:T(8,128)}, f32[252,128]{1,0:T(8,128)}) fusion(f32[252,256]{1,0:T(8,128)S(1)} %fusion.100), kind=kLoop, calls=%fused_computation.475 | loop fusion | bytes 516096 | tf_op jit(solution)/shard_map/slice | solution.py:259
  34.3 9.8 %shard_map.159 = (f32[252,128]{1,0:T(8,128)}, f32[252,128]{1,0:T(8,128)}, f32[9,84,128]{2,1,0:T(8,128)}) custom-call(f32[252,128]{1,0:T(8,128)} %get-tuple-element.167.refs_0_, f32[252,128]{1,0:T(8,128)} %get-tuple-element.166.refs_1_, f32[9,84,128]{2,1,0:T(8,128)} %copy-done.2, f32[3,84,84]{2,1,0:T(8,128)} %bitcast.623, f32[3,81,128]{2,1,0:T(8,128)} %refs_4_.3), custom_call_target="tpu_custom_call" | custom-call | tf_op jit(solution)/shard_map/pallas_call | solution.py:143
  44.1 1.9 %fusion = f32[252,512]{1,0:T(8,128)S(1)} fusion(f32[252,128]{1,0:T(8,128)} %get-tuple-element.13, f32[252,128]{1,0:T(8,128)} %get-tuple-element.12, f32[252,512]{1,0:T(8,128)S(1)} %bitcast.617, s32[512]{0:T(512)S(1)} %bitcast.644), kind=kOutput, calls=%fused_computation.3 | convolution fusion | flops 1189865472 | bytes 1292288 | tf_op jit(solution)/shard_map/dot_general | solution.py:262
  46.0 0.2 reshape.288
  46.2 0.8 %convolution_bitcast_fusion = f32[3,9,28,4,128]{4,2,3,1,0:T(8,128)S(1)} fusion(f32[9,28,4,128]{3,2,1,0:T(4,128)S(1)} %reshape.288, f32[3,28,28]{2,1,0:T(8,128)S(1)} %copy-done), kind=kOutput, calls=%fused_computation.5 | convolution fusion | flops 65028096 | bytes 2073792 | tf_op jit(solution)/shard_map/rts,qsic->rqtic/dot_general | solution.py:52
  47.0 0.2 fusion.18
  47.2 0.0 copy-start.18
  47.4 0.9 %copy-done.14 = f32[9,84,128]{2,1,0:T(8,128)S(1)} copy-done((f32[9,84,128]{2,1,0:T(8,128)S(1)}, f32[9,84,128]{2,1,0:T(8,128)}, u32[]{:S(2)}) %copy-start.14) | copy-done | bytes 387096
  48.2 1.3 %broadcast_multiply_fusion = (f32[9,84,128]{2,1,0:T(8,128)S(1)}, f32[9,84,128]{2,1,0:T(8,128)S(1)}, f32[9,84,128]{2,1,0:T(8,128)S(1)}) fusion(f32[84]{0:T(128)S(1)} %copy-done.18, f32[9,84,128]{2,1,0:T(8,128)S(1)} %fusion.2, f32[4,84,28]{1,0,2:T(4,128)S(1)} %copy-done.16, f32[28,4,128]{2,0,1:T(8,128)S(1)} %get-tuple-element.140, ...), kind=kOutput, calls=%fused_computation.214 | convolution fusion | flops 69931008 | bytes 3337296 | tf_op jit(solution)/shard_map/ibt,qtic->qbc/dot_general | solution.py:265
  49.6 0.1 copy.137
  49.7 1.0 %copy-done.5 = f32[2,1,9,84,128]{4,1,3,2,0:T(1,128)S(1)} copy-done((f32[2,1,9,84,128]{4,1,3,2,0:T(1,128)S(1)}, f32[2,1,9,84,128]{4,1,3,2,0:T(1,128)}, u32[]{:S(2)}) %copy-start.5) | copy-done | bytes 774168
  50.7 0.1 fusion.209
  50.8 0.1 reshape.307
  50.8 1.0 %multiply_reduce_fusion = f32[3,128]{1,0:T(4,128)S(1)} fusion(f32[9,84,128]{2,0,1:T(8,128)S(1)} %copy.137, f32[1,1,9,84,128]{4,1,3,2,0:T(1,128)S(1)} %get-tuple-element.128, f32[3,9,9,1]{2,1,0,3:T(8,128)S(1)} %reshape.307), kind=kOutput, calls=%fused_computation | convolution fusion | flops 16256640 | bytes 776652 | tf_op jit(solution)/shard_map/pqr,rbc->pqbc/dot_general | solution.py:268
  51.9 0.1 copy.134
  52.0 1.0 %multiply_reduce_fusion.1 = f32[3,128]{1,0:T(4,128)S(1)} fusion(f32[9,84,128]{2,0,1:T(8,128)S(1)} %copy.134, f32[1,1,9,84,128]{4,1,3,2,0:T(1,128)S(1)} %get-tuple-element.129, f32[3,9,9,1]{2,1,0,3:T(8,128)S(1)} %reshape.307), kind=kOutput, calls=%fused_computation.1 | convolution fusion | flops 16256640 | bytes 776652 | tf_op jit(solution)/shard_map/pqr,rbc->pqbc/dot_general | solution.py:268
  53.0 0.4 fusion.16
  53.6 0.0 copy-start.9
  53.6 0.6 copy-done.9
  54.2 11.3 %shard_map.160 = f32[11,3,128]{2,1,0:T(4,128)} custom-call(f32[11,3,128]{2,1,0:T(4,128)} %copy-done.9), custom_call_target="tpu_custom_call" | custom-call | tf_op jit(solution)/shard_map/pallas_call | solution.py:196
  65.5 0.8 %reduce_sum.31 = f32[3,128]{1,0:T(4,128)S(1)} reduce(f32[11,3,128]{2,1,0:T(4,128)} %shard_map.160, f32[]{:T(128)} %constant.74.clone.1), dimensions={0}, to_apply=%region_2.3 | reduce | flops 3840 | bytes 18436 | tf_op jit(solution)/shard_map/reduce_sum | solution.py:207
  66.2 0.6 copy.141
  66.8 1.1 %copy.140 = f32[1,9,84,128]{3,0,2,1:T(1,128)} copy(f32[1,9,84,128]{3,2,1,0:T(8,128)S(1)} %bitcast.624) | data formatting | bytes 774144
  (68 shorter events, 0.7 us)
Async XLA Ops:
  0.6 23.0 %copy-start = (f32[3,28,28]{2,1,0:T(8,128)S(1)}, f32[3,28,28]{2,1,0:T(8,128)}, u32[]{:S(2)}) copy-start(f32[3,28,28]{2,1,0:T(8,128)} %param.23) | copy-start | bytes 28228
  0.6 1.2 %copy-start.3 = (f32[1,9,84,128]{3,0,2,1:T(1,128)S(1)}, f32[1,9,84,128]{3,0,2,1:T(1,128)}, u32[]{:S(2)}) copy-start(f32[1,9,84,128]{3,0,2,1:T(1,128)} %param.15) | copy-start | bytes 1161220
  3.5 0.9 %copy-start.4 = (f32[3,84,84]{2,1,0:T(8,128)S(1)}, f32[3,84,84]{2,1,0:T(8,128)}, u32[]{:S(2)}) copy-start(f32[3,84,84]{2,1,0:T(8,128)} %param.20) | copy-start | bytes 254020
  6.2 2.3 %copy-start.8 = (f32[112,84]{0,1:T(8,128)S(1)}, f32[112,84]{0,1:T(8,128)}, u32[]{:S(2)}) copy-start(f32[112,84]{0,1:T(8,128)} %param.21) | copy-start | bytes 112900
  8.5 1.0 %copy-start.1 = (f32[9,84,128]{2,1,0:T(8,128)}, f32[9,84,128]{2,1,0:T(8,128)S(1)}, u32[]{:S(2)}) copy-start(f32[9,84,128]{2,1,0:T(8,128)S(1)} %fusion.104.refs_2_) | copy-start | bytes 1161220
  9.1 0.7 %copy-start.12 = (s32[2,128]{1,0:T(2,128)S(1)}, s32[2,128]{1,0:T(2,128)}, u32[]{:S(2)}) copy-start(s32[2,128]{1,0:T(2,128)} %param.28) | copy-start | bytes 3076
  9.5 12.0 %copy-start.17 = (s32[4,128]{1,0:T(4,128)S(1)}, s32[4,128]{1,0:T(4,128)}, u32[]{:S(2)}) copy-start(s32[4,128]{1,0:T(4,128)} %param.27) | copy-start | bytes 6148
  23.5 1.1 %copy-start.10 = (s32[4,128]{1,0:T(4,128)S(1)}, s32[4,128]{1,0:T(4,128)}, u32[]{:S(2)}) copy-start(s32[4,128]{1,0:T(4,128)} %param.24) | copy-start | bytes 6148
  24.8 0.9 %copy-start.6 = (f32[4,81,128]{2,0,1:T(4,128)S(1)}, f32[4,81,128]{2,0,1:T(4,128)}, u32[]{:S(2)}) copy-start(f32[4,81,128]{2,0,1:T(4,128)} %param.19) | copy-start | bytes 497668
  24.8 1.0 %copy-start.7 = (f32[4,81,128]{2,0,1:T(4,128)S(1)}, f32[4,81,128]{2,0,1:T(4,128)}, u32[]{:S(2)}) copy-start(f32[4,81,128]{2,0,1:T(4,128)} %param.18) | copy-start | bytes 497668
  24.8 1.2 %copy-start.15 = (f32[9,84,128]{2,1,0:T(8,128)S(1)}, f32[9,84,128]{2,1,0:T(8,128)}, u32[]{:S(2)}) copy-start(f32[9,84,128]{2,1,0:T(8,128)} %get-tuple-element.8) | copy-start | bytes 1161220
  24.8 1.1 %copy-start.16 = (f32[4,84,28]{1,0,2:T(4,128)S(1)}, f32[4,84,28]{1,0,2:T(4,128)}, u32[]{:S(2)}) copy-start(f32[4,84,28]{1,0,2:T(4,128)} %param.22) | copy-start | bytes 112900
  32.2 0.9 %copy-start.2 = (f32[9,84,128]{2,1,0:T(8,128)}, f32[9,84,128]{2,1,0:T(8,128)S(1)}, u32[]{:S(2)}) copy-start(f32[9,84,128]{2,1,0:T(8,128)S(1)} %multiply_add_fusion.refs_2_) | copy-start | bytes 1161220
  47.2 1.0 %copy-start.14 = (f32[9,84,128]{2,1,0:T(8,128)S(1)}, f32[9,84,128]{2,1,0:T(8,128)}, u32[]{:S(2)}) copy-start(f32[9,84,128]{2,1,0:T(8,128)} %get-tuple-element.11) | copy-start | bytes 1161220
  47.2 1.0 %copy-start.18 = (f32[84]{0:T(128)S(1)}, f32[84]{0:T(128)}, u32[]{:S(2)}) copy-start(f32[84]{0:T(128)} %param.25) | copy-start | bytes 1012
  49.5 1.1 %copy-start.5 = (f32[2,1,9,84,128]{4,1,3,2,0:T(1,128)S(1)}, f32[2,1,9,84,128]{4,1,3,2,0:T(1,128)}, u32[]{:S(2)}) copy-start(f32[2,1,9,84,128]{4,1,3,2,0:T(1,128)} %param.16) | copy-start | bytes 2322436
  49.6 1.2 %copy-start.11 = (f32[3,81]{1,0:T(4,128)S(1)}, f32[3,81]{1,0:T(4,128)}, u32[]{:S(2)}) copy-start(f32[3,81]{1,0:T(4,128)} %param.26) | copy-start | bytes 2920
  51.9 1.1 %copy-start.13 = (s32[128]{0:T(128)S(1)}, s32[128]{0:T(128)}, u32[]{:S(2)}) copy-start(s32[128]{0:T(128)} %param.29) | copy-start | bytes 1540
  53.6 0.6 copy-start.9

commit v5 on v4

--- a/solution.py
+++ b/solution.py
@@ -157,14 +157,38 @@
 def scatter_kernel(offsets, group_count, curve_count, chunks, received, send_sem, recv_sem):
     group = lax.axis_index("grp")
     me = lax.axis_index("curve")
+    sides = {-1: me > 0, 0: None, 1: me < curve_count - 1}
     targets = [
         (lax.rem(group + shift_group, group_count), lax.rem(me + shift_curve + curve_count, curve_count))
         for shift_group, shift_curve in offsets
     ]
+
+    def maybe(side, action):
+        if sides[side] is None:
+            action()
+        else:
+            pl.when(sides[side])(action)
+
     barrier = pltpu.get_barrier_semaphore()
-    for target in targets:
-        pl.semaphore_signal(barrier, inc=1, device_id=target, device_id_type=pl.DeviceIdType.MESH)
-    pl.semaphore_wait(barrier, len(offsets))
+    for (shift_group, shift_curve), target in zip(offsets, targets):
+        maybe(
+            shift_curve,
+            lambda target=target: pl.semaphore_signal(
+                barrier, inc=1, device_id=target, device_id_type=pl.DeviceIdType.MESH
+            ),
+        )
+    for index, (shift_group, shift_curve) in enumerate(offsets):
+        if shift_curve != 0:
+
+            def clear(index=index):
+                received[index] = jnp.zeros_like(received[index])
+
+            pl.when(jnp.logical_not(sides[-shift_curve]))(clear)
+    has_left = (me + curve_count - 1) // curve_count
+    has_right = (2 * curve_count - 2 - me) // curve_count
+    per_side = sum(1 for _, shift_curve in offsets if shift_curve == 1)
+    steady = sum(1 for _, shift_curve in offsets if shift_curve == 0)
+    pl.semaphore_wait(barrier, steady + per_side * (has_left + has_right))
     copies = [
         pltpu.make_async_remote_copy(
             src_ref=chunks.at[index],
@@ -176,10 +200,11 @@
         )
         for index, target in enumerate(targets)
     ]
-    for copy in copies:
-        copy.start()
-    for copy in copies:
-        copy.wait()
+    for (shift_group, shift_curve), copy in zip(offsets, copies):
+        maybe(shift_curve, copy.start)
+    for (shift_group, shift_curve), copy in zip(offsets, copies):
+        maybe(shift_curve, copy.wait_send)
+        maybe(-shift_curve, copy.wait_recv)
 
 
 def scatter_tiles(partial):

time: 68.4 us -> 68.4 us (level)
  no operation moved by 1% of the time
where the time goes in v5:
time: 68.4 us; the launch traced here: 67.9 us
  Pallas kernels  30.9 us (45%)
  matrix products  18 us (26%)
  local copies, waits for them, and re-layouts  11.9 us (17%)
  other arithmetic  5.78 us (8%)
  between operations  1.39 us (2%)
    pallas_call x2, Pallas kernels, exchange(): pl.pallas_call(lambda *refs: exchange_kernel(count, *refs), out_shape=(ja...  19.6 us
    pallas_call x1, Pallas kernels, scatter_tiles(): pl.pallas_call(lambda *refs: scatter_kernel(offsets, group_count, curve_c...  11.3 us
    unnamed x57, local copies, waits for them, and re-layouts  7.39 us
    dot_general x4, matrix products, predictor(): moved = jnp.einsum('dab,qbc->dqac', stiffness, derivative, precision=DENSE)  5.82 us
    add x2, other arithmetic, predictor(): integral = integral + factor * derivative  4.56 us
    dot_general x2, matrix products, on_device(): jnp.dot(extended, gather_oh, precision=PRECISE)  3.79 us
    dot_general x2, matrix products, on_device(): lifted = jnp.einsum('ibt,qtic->qbc', lifting, face_flux, precision=DENSE)  2.57 us
    dot_general x2, matrix products, on_device(): jnp.einsum('pqr,rbc->pqbc', mix, forward[time_step, 0], precision=DENSE)  2.04 us

profile of v5, /device:TPU:103, one launch (start us, length us, event | category | flops | bytes accessed | tf_op | source)
XLA Modules:
  0.0 67.9 jit_solution(9458676558832320741)
XLA Ops:
  0.6 0.0 copy-start
  0.7 0.9 %fusion.212 = (f32[1,81,128]{2,1,0:T(8,128)S(1)}, f32[1,81,128]{2,1,0:T(8,128)S(1)}, f32[1,81,128]{2,1,0:T(8,128)S(1)}) fusion(f32[3,81,128]{2,1,0:T(8,128)} %refs_4_.3), kind=kLoop, calls=%fused_computation.477 | loop fusion | bytes 248832 | tf_op jit(solution)/shard_map/slice | solution.py:28
  1.9 1.6 %convolution_bitcast_fusion.5 = f32[3,9,84,128]{3,2,0,1:T(8,128)S(1)} fusion(f32[1,9,84,128]{3,0,2,1:T(1,128)S(1)} %copy-done.3, f32[3,84,84]{2,1,0:T(8,128)} %param.20), kind=kOutput, calls=%fused_computation.10 | convolution fusion | flops 146313216 | bytes 1632960 | tf_op jit(solution)/shard_map/dab,qbc->dqac/dot_general | solution.py:39
  3.5 0.0 copy-start.4
  3.5 0.1 slice_bitcast_fusion.149
  3.6 0.8 %copy-done.4 = f32[3,84,84]{2,1,0:T(8,128)S(1)} copy-done((f32[3,84,84]{2,1,0:T(8,128)S(1)}, f32[3,84,84]{2,1,0:T(8,128)}, u32[]{:S(2)}) %copy-start.4) | copy-done | bytes 84696
  4.4 1.8 %convolution_bitcast_fusion.4 = f32[3,9,84,128]{3,2,0,1:T(8,128)S(1)} fusion(f32[3,84,84]{2,1,0:T(8,128)S(1)} %copy-done.4, f32[84,128]{1,0:T(8,128)S(1)} %get-tuple-element.102, f32[9,128]{1,0:T(8,128)S(1)} %get-tuple-element.226, f32[84,128]{1,0:T(8,128)S(1)} %get-tuple-element.103, f32[9,128]{1,0:T(8,128)S(1)} %get-tuple-element.227, ...), kind=kOutput, calls=%fused_computation.9 | convolution fusion | flops 151441920 | bytes 2531520 | tf_op jit(solution)/shard_map/dab,qbc->dqac/dot_general | solution.py:39
  6.1 0.1 slice_bitcast_fusion.122
  6.2 0.0 copy-start.8
  6.3 2.3 %fusion.104.refs_2_ = f32[9,84,128]{2,1,0:T(8,128)S(1)} fusion(f32[1,9,84,128]{3,0,2,1:T(1,128)S(1)} %copy-done.3, f32[84,128]{1,0:T(8,128)S(1)} %get-tuple-element.75, f32[84,128]{1,0:T(8,128)S(1)} %get-tuple-element.76, f32[84,128]{1,0:T(8,128)S(1)} %get-tuple-element.77, f32[84,128]{1,0:T(8,128)S(1)} %get-tuple-element.78, ...), kind=kLoop, calls=%fused_computation.129 | loop fusion | flops 10741248 | bytes 3220992 | tf_op jit(solution)/shard_map/add | solution.py:42
  8.6 0.1 copy.123
  8.7 0.4 convolution_bitcast_fusion.7
  9.1 0.0 copy-start.12
  9.1 0.3 copy.124
  9.4 0.1 pad.8
  9.5 0.0 copy-start.17
  9.6 0.2 copy-done.12
  9.8 0.4 fusion.101
  10.2 0.7 %fusion.211 = (f32[252,128]{1,0:T(8,128)}, f32[252,128]{1,0:T(8,128)}) fusion(f32[252,256]{1,0:T(8,128)S(1)} %fusion.101), kind=kLoop, calls=%fused_computation.476 | loop fusion | bytes 516096 | tf_op jit(solution)/shard_map/slice | solution.py:284
  10.9 0.8 %copy.125 = f32[3,84,84]{1,2,0:T(8,128)} copy(f32[3,84,84]{2,1,0:T(8,128)S(1)} %copy-done.4) | data formatting | bytes 169344 | tf_op args[5]
  11.7 9.8 %shard_map.158 = (f32[252,128]{1,0:T(8,128)}, f32[252,128]{1,0:T(8,128)}, f32[9,84,128]{2,1,0:T(8,128)}) custom-call(f32[252,128]{1,0:T(8,128)} %get-tuple-element.169.refs_0_, f32[252,128]{1,0:T(8,128)} %get-tuple-element.168.refs_1_, f32[9,84,128]{2,1,0:T(8,128)} %copy-done.1, f32[3,84,84]{2,1,0:T(8,128)} %bitcast.622, f32[3,81,128]{2,1,0:T(8,128)} %refs_4_.3), custom_call_target="tpu_custom_call" | custom-call | tf_op jit(solution)/shard_map/pallas_call | solution.py:143
  21.6 1.9 %fusion.1 = f32[252,512]{1,0:T(8,128)S(1)} fusion(f32[252,128]{1,0:T(8,128)} %get-tuple-element.10, f32[252,128]{1,0:T(8,128)} %get-tuple-element.9, f32[252,512]{1,0:T(8,128)S(1)} %bitcast.615, s32[512]{0:T(512)S(1)} %bitcast.643), kind=kOutput, calls=%fused_computation.4 | convolution fusion | flops 1189865472 | bytes 1292288 | tf_op jit(solution)/shard_map/dot_general | solution.py:287
  23.5 0.0 copy-start.10
  23.5 0.2 reshape.286
  23.7 0.8 %convolution_bitcast_fusion.1 = f32[3,9,28,4,128]{4,2,0,3,1:T(8,128)S(1)} fusion(f32[9,28,4,128,1]{3,2,1,0,4:T(4,128)S(1)} %bitcast.613, f32[3,28,28]{2,1,0:T(8,128)S(1)} %copy-done), kind=kOutput, calls=%fused_computation.6 | convolution fusion | flops 65028096 | bytes 2073792 | tf_op jit(solution)/shard_map/rts,qsic->rqtic/dot_general | solution.py:52
  24.5 0.2 fusion.23
  24.8 0.0 copy-start.16
  24.9 0.8 %copy-done.6 = f32[4,81,128]{2,0,1:T(4,128)S(1)} copy-done((f32[4,81,128]{2,0,1:T(4,128)S(1)}, f32[4,81,128]{2,0,1:T(4,128)}, u32[]{:S(2)}) %copy-start.6) | copy-done | bytes 165912
  25.7 0.1 copy-done.7
  25.8 0.1 slice_bitcast_fusion.158
  25.8 0.1 copy-done.15
  25.9 1.3 %fusion.2 = f32[9,84,128]{2,1,0:T(8,128)S(1)} fusion(f32[9,84,128]{2,1,0:T(8,128)S(1)} %copy-done.15, f32[1,9,84,128]{3,0,2,1:T(1,128)S(1)} %copy-done.3, f32[28,4,128]{2,0,1:T(8,128)S(1)} %get-tuple-element.158, f32[9,4,128]{2,1,0:T(4,128)S(1)} %get-tuple-element.180, f32[28,4,128]{2,0,1:T(8,128)S(1)} %get-tuple-element.159, ...), kind=kOutput, calls=%fused_computation.15 | convolution fusion | flops 69737472 | bytes 2562816 | tf_op jit(solution)/shard_map/ibt,qtic->qbc/dot_general | solution.py:290
  27.2 0.7 convolution_bitcast_fusion.3
  27.9 0.1 slice_bitcast_fusion.95
  28.0 1.8 %convolution_bitcast_fusion.2 = f32[3,9,84,128]{3,2,0,1:T(8,128)S(1)} fusion(f32[3,84,84]{2,1,0:T(8,128)S(1)} %copy-done.4, f32[84,128]{1,0:T(8,128)S(1)} %get-tuple-element.48, f32[84,128]{1,0:T(8,128)S(1)} %get-tuple-element.49, f32[84,128]{1,0:T(8,128)S(1)} %get-tuple-element.50, f32[84,128]{1,0:T(8,128)S(1)} %get-tuple-element.51, ...), kind=kOutput, calls=%fused_computation.7 | convolution fusion | flops 151441920 | bytes 2531520 | tf_op jit(solution)/shard_map/dab,qbc->dqac/dot_general | solution.py:39
  29.8 0.1 slice_bitcast_fusion.68
  29.9 2.3 %multiply_add_fusion.refs_2_ = f32[9,84,128]{2,1,0:T(8,128)S(1)} fusion(f32[9,84,128]{2,1,0:T(8,128)S(1)} %fusion.2, f32[84,128]{1,0:T(8,128)S(1)} %get-tuple-element.21, f32[84,128]{1,0:T(8,128)S(1)} %get-tuple-element.22, f32[84,128]{1,0:T(8,128)S(1)} %get-tuple-element.23, f32[84,128]{1,0:T(8,128)S(1)} %get-tuple-element.24, ...), kind=kLoop, calls=%fused_computation.135 | loop fusion | flops 10741248 | bytes 3220992 | tf_op jit(solution)/shard_map/add | solution.py:42
  32.2 0.4 convolution_bitcast_fusion.6
  32.6 0.3 copy.130
  32.9 0.1 pad.9
  33.1 0.4 fusion.100
  33.5 0.7 %fusion.210 = (f32[252,128]{1,0:T(8,128)}, f32[252,128]{1,0:T(8,128)}) fusion(f32[252,256]{1,0:T(8,128)S(1)} %fusion.100), kind=kLoop, calls=%fused_computation.475 | loop fusion | bytes 516096 | tf_op jit(solution)/shard_map/slice | solution.py:284
  34.3 9.8 %shard_map.159 = (f32[252,128]{1,0:T(8,128)}, f32[252,128]{1,0:T(8,128)}, f32[9,84,128]{2,1,0:T(8,128)}) custom-call(f32[252,128]{1,0:T(8,128)} %get-tuple-element.167.refs_0_, f32[252,128]{1,0:T(8,128)} %get-tuple-element.166.refs_1_, f32[9,84,128]{2,1,0:T(8,128)} %copy-done.2, f32[3,84,84]{2,1,0:T(8,128)} %bitcast.623, f32[3,81,128]{2,1,0:T(8,128)} %refs_4_.3), custom_call_target="tpu_custom_call" | custom-call | tf_op jit(solution)/shard_map/pallas_call | solution.py:143
  44.1 1.9 %fusion = f32[252,512]{1,0:T(8,128)S(1)} fusion(f32[252,128]{1,0:T(8,128)} %get-tuple-element.13, f32[252,128]{1,0:T(8,128)} %get-tuple-element.12, f32[252,512]{1,0:T(8,128)S(1)} %bitcast.617, s32[512]{0:T(512)S(1)} %bitcast.644), kind=kOutput, calls=%fused_computation.3 | convolution fusion | flops 1189865472 | bytes 1292288 | tf_op jit(solution)/shard_map/dot_general | solution.py:287
  46.0 0.2 reshape.288
  46.2 0.8 %convolution_bitcast_fusion = f32[3,9,28,4,128]{4,2,3,1,0:T(8,128)S(1)} fusion(f32[9,28,4,128]{3,2,1,0:T(4,128)S(1)} %reshape.288, f32[3,28,28]{2,1,0:T(8,128)S(1)} %copy-done), kind=kOutput, calls=%fused_computation.5 | convolution fusion | flops 65028096 | bytes 2073792 | tf_op jit(solution)/shard_map/rts,qsic->rqtic/dot_general | solution.py:52
  47.0 0.2 fusion.18
  47.2 0.0 copy-start.18
  47.4 0.9 %copy-done.14 = f32[9,84,128]{2,1,0:T(8,128)S(1)} copy-done((f32[9,84,128]{2,1,0:T(8,128)S(1)}, f32[9,84,128]{2,1,0:T(8,128)}, u32[]{:S(2)}) %copy-start.14) | copy-done | bytes 387096
  48.2 1.3 %broadcast_multiply_fusion = (f32[9,84,128]{2,1,0:T(8,128)S(1)}, f32[9,84,128]{2,1,0:T(8,128)S(1)}, f32[9,84,128]{2,1,0:T(8,128)S(1)}) fusion(f32[84]{0:T(128)S(1)} %copy-done.18, f32[9,84,128]{2,1,0:T(8,128)S(1)} %fusion.2, f32[4,84,28]{1,0,2:T(4,128)S(1)} %copy-done.16, f32[28,4,128]{2,0,1:T(8,128)S(1)} %get-tuple-element.140, ...), kind=kOutput, calls=%fused_computation.214 | convolution fusion | flops 69931008 | bytes 3337296 | tf_op jit(solution)/shard_map/ibt,qtic->qbc/dot_general | solution.py:290
  49.6 0.1 copy.137
  49.7 1.0 %copy-done.5 = f32[2,1,9,84,128]{4,1,3,2,0:T(1,128)S(1)} copy-done((f32[2,1,9,84,128]{4,1,3,2,0:T(1,128)S(1)}, f32[2,1,9,84,128]{4,1,3,2,0:T(1,128)}, u32[]{:S(2)}) %copy-start.5) | copy-done | bytes 774168
  50.7 0.1 fusion.209
  50.8 0.1 reshape.307
  50.8 1.0 %multiply_reduce_fusion = f32[3,128]{1,0:T(4,128)S(1)} fusion(f32[9,84,128]{2,0,1:T(8,128)S(1)} %copy.137, f32[1,1,9,84,128]{4,1,3,2,0:T(1,128)S(1)} %get-tuple-element.128, f32[3,9,9,1]{2,1,0,3:T(8,128)S(1)} %reshape.307), kind=kOutput, calls=%fused_computation | convolution fusion | flops 16256640 | bytes 776652 | tf_op jit(solution)/shard_map/pqr,rbc->pqbc/dot_general | solution.py:293
  51.9 0.1 copy.134
  52.0 1.0 %multiply_reduce_fusion.1 = f32[3,128]{1,0:T(4,128)S(1)} fusion(f32[9,84,128]{2,0,1:T(8,128)S(1)} %copy.134, f32[1,1,9,84,128]{4,1,3,2,0:T(1,128)S(1)} %get-tuple-element.129, f32[3,9,9,1]{2,1,0,3:T(8,128)S(1)} %reshape.307), kind=kOutput, calls=%fused_computation.1 | convolution fusion | flops 16256640 | bytes 776652 | tf_op jit(solution)/shard_map/pqr,rbc->pqbc/dot_general | solution.py:293
  53.0 0.4 fusion.16
  53.6 0.0 copy-start.9
  53.6 0.6 copy-done.9
  54.2 11.3 %shard_map.160 = f32[11,3,128]{2,1,0:T(4,128)} custom-call(f32[11,3,128]{2,1,0:T(4,128)} %copy-done.9), custom_call_target="tpu_custom_call" | custom-call | tf_op jit(solution)/shard_map/pallas_call | solution.py:221
  65.5 0.8 %reduce_sum.31 = f32[3,128]{1,0:T(4,128)S(1)} reduce(f32[11,3,128]{2,1,0:T(4,128)} %shard_map.160, f32[]{:T(128)} %constant.74.clone.1), dimensions={0}, to_apply=%region_2.3 | reduce | flops 3840 | bytes 18436 | tf_op jit(solution)/shard_map/reduce_sum | solution.py:232
  66.2 0.6 copy.141
  66.8 1.1 %copy.140 = f32[1,9,84,128]{3,0,2,1:T(1,128)} copy(f32[1,9,84,128]{3,2,1,0:T(8,128)S(1)} %bitcast.624) | data formatting | bytes 774144
  (68 shorter events, 0.7 us)
Async XLA Ops:
  0.6 23.0 %copy-start = (f32[3,28,28]{2,1,0:T(8,128)S(1)}, f32[3,28,28]{2,1,0:T(8,128)}, u32[]{:S(2)}) copy-start(f32[3,28,28]{2,1,0:T(8,128)} %param.23) | copy-start | bytes 28228
  0.6 1.2 %copy-start.3 = (f32[1,9,84,128]{3,0,2,1:T(1,128)S(1)}, f32[1,9,84,128]{3,0,2,1:T(1,128)}, u32[]{:S(2)}) copy-start(f32[1,9,84,128]{3,0,2,1:T(1,128)} %param.15) | copy-start | bytes 1161220
  3.5 0.9 %copy-start.4 = (f32[3,84,84]{2,1,0:T(8,128)S(1)}, f32[3,84,84]{2,1,0:T(8,128)}, u32[]{:S(2)}) copy-start(f32[3,84,84]{2,1,0:T(8,128)} %param.20) | copy-start | bytes 254020
  6.2 2.3 %copy-start.8 = (f32[112,84]{0,1:T(8,128)S(1)}, f32[112,84]{0,1:T(8,128)}, u32[]{:S(2)}) copy-start(f32[112,84]{0,1:T(8,128)} %param.21) | copy-start | bytes 112900
  8.5 1.0 %copy-start.1 = (f32[9,84,128]{2,1,0:T(8,128)}, f32[9,84,128]{2,1,0:T(8,128)S(1)}, u32[]{:S(2)}) copy-start(f32[9,84,128]{2,1,0:T(8,128)S(1)} %fusion.104.refs_2_) | copy-start | bytes 1161220
  9.1 0.7 %copy-start.12 = (s32[2,128]{1,0:T(2,128)S(1)}, s32[2,128]{1,0:T(2,128)}, u32[]{:S(2)}) copy-start(s32[2,128]{1,0:T(2,128)} %param.28) | copy-start | bytes 3076
  9.5 12.0 %copy-start.17 = (s32[4,128]{1,0:T(4,128)S(1)}, s32[4,128]{1,0:T(4,128)}, u32[]{:S(2)}) copy-start(s32[4,128]{1,0:T(4,128)} %param.27) | copy-start | bytes 6148
  23.5 1.1 %copy-start.10 = (s32[4,128]{1,0:T(4,128)S(1)}, s32[4,128]{1,0:T(4,128)}, u32[]{:S(2)}) copy-start(s32[4,128]{1,0:T(4,128)} %param.24) | copy-start | bytes 6148
  24.8 0.9 %copy-start.6 = (f32[4,81,128]{2,0,1:T(4,128)S(1)}, f32[4,81,128]{2,0,1:T(4,128)}, u32[]{:S(2)}) copy-start(f32[4,81,128]{2,0,1:T(4,128)} %param.19) | copy-start | bytes 497668
  24.8 1.0 %copy-start.7 = (f32[4,81,128]{2,0,1:T(4,128)S(1)}, f32[4,81,128]{2,0,1:T(4,128)}, u32[]{:S(2)}) copy-start(f32[4,81,128]{2,0,1:T(4,128)} %param.18) | copy-start | bytes 497668
  24.8 1.2 %copy-start.15 = (f32[9,84,128]{2,1,0:T(8,128)S(1)}, f32[9,84,128]{2,1,0:T(8,128)}, u32[]{:S(2)}) copy-start(f32[9,84,128]{2,1,0:T(8,128)} %get-tuple-element.8) | copy-start | bytes 1161220
  24.8 1.1 %copy-start.16 = (f32[4,84,28]{1,0,2:T(4,128)S(1)}, f32[4,84,28]{1,0,2:T(4,128)}, u32[]{:S(2)}) copy-start(f32[4,84,28]{1,0,2:T(4,128)} %param.22) | copy-start | bytes 112900
  32.2 0.9 %copy-start.2 = (f32[9,84,128]{2,1,0:T(8,128)}, f32[9,84,128]{2,1,0:T(8,128)S(1)}, u32[]{:S(2)}) copy-start(f32[9,84,128]{2,1,0:T(8,128)S(1)} %multiply_add_fusion.refs_2_) | copy-start | bytes 1161220
  47.2 1.0 %copy-start.14 = (f32[9,84,128]{2,1,0:T(8,128)S(1)}, f32[9,84,128]{2,1,0:T(8,128)}, u32[]{:S(2)}) copy-start(f32[9,84,128]{2,1,0:T(8,128)} %get-tuple-element.11) | copy-start | bytes 1161220
  47.2 1.0 %copy-start.18 = (f32[84]{0:T(128)S(1)}, f32[84]{0:T(128)}, u32[]{:S(2)}) copy-start(f32[84]{0:T(128)} %param.25) | copy-start | bytes 1012
  49.5 1.1 %copy-start.5 = (f32[2,1,9,84,128]{4,1,3,2,0:T(1,128)S(1)}, f32[2,1,9,84,128]{4,1,3,2,0:T(1,128)}, u32[]{:S(2)}) copy-start(f32[2,1,9,84,128]{4,1,3,2,0:T(1,128)} %param.16) | copy-start | bytes 2322436
  49.6 1.2 %copy-start.11 = (f32[3,81]{1,0:T(4,128)S(1)}, f32[3,81]{1,0:T(4,128)}, u32[]{:S(2)}) copy-start(f32[3,81]{1,0:T(4,128)} %param.26) | copy-start | bytes 2920
  51.9 1.1 %copy-start.13 = (s32[128]{0:T(128)S(1)}, s32[128]{0:T(128)}, u32[]{:S(2)}) copy-start(s32[128]{0:T(128)} %param.29) | copy-start | bytes 1540
  53.6 0.6 copy-start.9
